TPU v7x, 32 devices: a whole 2x2x4 slice. The times are simulated.
32 devices in a mesh: dp: 16 (over z, x, core), tensor: 2 (over y).
Axes of the slice: x: 2, y: 2, z: 4, core: 2. Of those that a mesh axis runs over, the one named last changes fastest.
Arguments:
- inputs: float32 [64, 320, 1024], P(('dp', 'tensor')), may hold values from -6 to 6
- key_mask: int32 [64, 256], P('dp'), may hold values 0 or 1
- ln1_gain: float32 [1024], P('dp'), may hold values from 0.1 to 1.9
- ln1_bias: float32 [1024], P('dp'), may hold values from -1.8 to 1.8
- w_qkv: float32 [3, 1024, 1024], P(None, 'dp', 'tensor'), may hold values from -0.1875 to 0.1875
- qv_bias: float32 [2, 1024], P(None, 'dp'), may hold values from -0.6 to 0.6
- w_proj: float32 [1024, 1024], P('tensor', 'dp'), may hold values from -3.5 to 3.5
- proj_bias: float32 [1024], P('dp'), may hold values from -1.8 to 1.8
- ln2_gain: float32 [1024], P('dp'), may hold values from 0.1 to 1.9
- ln2_bias: float32 [1024], P('dp'), may hold values from -1.8 to 1.8
- w_fc1: float32 [1024, 4096], P('dp', 'tensor'), may hold values from -0.1875 to 0.1875
- fc1_bias: float32 [4096], P('dp'), may hold values from -3 to 3
- w_fc2: float32 [4096, 1024], P('tensor', 'dp'), may hold values from -0.09375 to 0.09375
- fc2_bias: float32 [1024], P('dp'), may hold values from -1.8 to 1.8
- out_grad: float32 [64, 320, 1024], P(('dp', 'tensor')), may hold values from -6 to 6
Outputs:
- activations: float32 [64, 320, 1024], P(('dp', 'tensor'))
- input_grad: float32 [64, 320, 1024], P(('dp', 'tensor'))
- ln1_gain_grad: float32 [1024], P('dp')
- ln1_bias_grad: float32 [1024], P('dp')
- w_qkv_grad: float32 [3, 1024, 1024], P(None, 'dp', 'tensor')
- qv_bias_grad: float32 [2, 1024], P(None, 'dp')
- w_proj_grad: float32 [1024, 1024], P('tensor', 'dp')
- proj_bias_grad: float32 [1024], P('dp')
- ln2_gain_grad: float32 [1024], P('dp')
- ln2_bias_grad: float32 [1024], P('dp')
- w_fc1_grad: float32 [1024, 4096], P('dp', 'tensor')
- fc1_bias_grad: float32 [4096], P('dp')
- w_fc2_grad: float32 [4096, 1024], P('tensor', 'dp')
- fc2_bias_grad: float32 [1024], P('dp')
All inputs are finite; a program needn't handle non-finite values. No bound on the sum of `key_mask` on one device may be relied on, other than what follows from the above.
Results may differ from a plain program's by a relative error of at most 0.015.
Values may be sent and summed in bfloat16 or wider, within the bound.
No kernel may reach another device: no remote copies, remote signals or barrier semaphores. Data moves between devices by JAX's collectives and lax.ppermute only.
A program may use at most 192 MiB of HBM per device.

v0:
```python
import jax
import jax.numpy as jnp
from jax import lax
from jax.sharding import PartitionSpec as P

HEAD_DIM = 64


norm_eps = 1e-06
masked_score = -1e30


def layer_norm(row_data, gain_vec, shift_vec):
    center = row_data - jnp.mean(row_data, axis=-1, keepdims=True)
    spread = jnp.mean(center * center, axis=-1, keepdims=True)
    return center * lax.rsqrt(spread + norm_eps) * gain_vec + shift_vec


def gelu_exact(values):
    return jax.nn.gelu(values, approximate=False)


def spread_rows(values):
    return lax.all_gather(values, "tensor", axis=0, tiled=True)


def fold_rows(values):
    return lax.psum_scatter(
        values.astype(jnp.bfloat16), "tensor", scatter_dimension=0, tiled=True
    ).astype(jnp.float32)


def spread_grads(values):
    return lax.all_gather(values, "tensor", axis=0, tiled=True)


def fold_grads(values):
    return lax.psum_scatter(
        values.astype(jnp.bfloat16), "tensor", scatter_dimension=0, tiled=True
    ).astype(jnp.float32)


def unpack(gathered, tensor_rank, half_width, half_hidden):
    (
        gain_one,
        bias_one,
        qkv_w,
        qv_b,
        proj_w,
        proj_b,
        gain_two,
        bias_two,
        fc1_w,
        fc1_b,
        fc2_w,
        fc2_b,
    ) = gathered
    qv_local = lax.dynamic_slice_in_dim(
        qv_b.astype(jnp.float32), tensor_rank * half_width, half_width, 1
    )
    fc1_local = lax.dynamic_slice_in_dim(
        fc1_b.astype(jnp.float32), tensor_rank * half_hidden, half_hidden, 0
    )
    return (
        gain_one.astype(jnp.float32),
        bias_one.astype(jnp.float32),
        qkv_w,
        qv_local,
        proj_w,
        proj_b.astype(jnp.float32),
        gain_two.astype(jnp.float32),
        bias_two.astype(jnp.float32),
        fc1_w,
        fc1_local,
        fc2_w,
        fc2_b.astype(jnp.float32),
    )


def shards(
    inputs,
    key_mask,
    ln1_gain,
    ln1_bias,
    w_qkv,
    qv_bias,
    w_proj,
    proj_bias,
    ln2_gain,
    ln2_bias,
    w_fc1,
    fc1_bias,
    w_fc2,
    fc2_bias,
    out_grad,
):
    tensor_rank = lax.axis_index("tensor")
    tensor_count = lax.axis_size("tensor")
    seq_len = inputs.shape[1]
    images = key_mask.shape[0]
    half_width = w_qkv.shape[2]
    half_hidden = w_fc1.shape[1]
    local_heads = half_width // HEAD_DIM
    scale_factor = HEAD_DIM ** (-0.5)
    ln1_gain_bf = ln1_gain.astype(jnp.bfloat16)
    ln1_bias_bf = ln1_bias.astype(jnp.bfloat16)
    w_qkv_bf = w_qkv.astype(jnp.bfloat16)
    qv_bias_bf = qv_bias.astype(jnp.bfloat16)
    w_proj_bf = w_proj.astype(jnp.bfloat16)
    proj_bias_bf = proj_bias.astype(jnp.bfloat16)
    ln2_gain_bf = ln2_gain.astype(jnp.bfloat16)
    ln2_bias_bf = ln2_bias.astype(jnp.bfloat16)
    w_fc1_bf = w_fc1.astype(jnp.bfloat16)
    fc1_bias_bf = fc1_bias.astype(jnp.bfloat16)
    w_fc2_bf = w_fc2.astype(jnp.bfloat16)
    fc2_bias_bf = fc2_bias.astype(jnp.bfloat16)
    gathered = (
        lax.all_gather(ln1_gain_bf, "dp", axis=0, tiled=True),
        lax.all_gather(ln1_bias_bf, "dp", axis=0, tiled=True),
        lax.all_gather(w_qkv_bf, "dp", axis=1, tiled=True),
        lax.all_gather(qv_bias_bf, "dp", axis=1, tiled=True),
        lax.all_gather(w_proj_bf, "dp", axis=1, tiled=True),
        lax.all_gather(proj_bias_bf, "dp", axis=0, tiled=True),
        lax.all_gather(ln2_gain_bf, "dp", axis=0, tiled=True),
        lax.all_gather(ln2_bias_bf, "dp", axis=0, tiled=True),
        lax.all_gather(w_fc1_bf, "dp", axis=0, tiled=True),
        lax.all_gather(fc1_bias_bf, "dp", axis=0, tiled=True),
        lax.all_gather(w_fc2_bf, "dp", axis=1, tiled=True),
        lax.all_gather(fc2_bias_bf, "dp", axis=0, tiled=True),
    )
    forward_params = unpack(gathered, tensor_rank, half_width, half_hidden)
    (
        gain_one,
        bias_one,
        qkv_w,
        qv_b,
        proj_w,
        proj_b,
        gain_two,
        bias_two,
        fc1_w,
        fc1_b,
        fc2_w,
        fc2_b,
    ) = forward_params
    buffer_len = seq_len - key_mask.shape[1]
    visible = jnp.concatenate([jnp.ones((images, buffer_len), jnp.int32), key_mask], axis=1) > 0
    normed_one = spread_rows(layer_norm(inputs, gain_one, bias_one).astype(jnp.bfloat16))
    projected = jnp.einsum("bsd,cde->cbse", normed_one, qkv_w, preferred_element_type=jnp.float32)
    queries = (projected[0] + qv_b[0]).astype(jnp.bfloat16)
    key_rows = projected[1].astype(jnp.bfloat16)
    value_rows = (projected[2] + qv_b[1]).astype(jnp.bfloat16)
    pair_size = 2
    blocks = images // pair_size

    def by_heads(values):
        return values.reshape(blocks, pair_size, seq_len, local_heads, HEAD_DIM)

    query_blk = by_heads(queries)
    key_blk = by_heads(key_rows)
    value_blk = by_heads(value_rows)
    seen_blk = visible.reshape(blocks, pair_size, seq_len)

    def score_block(query_part, key_part, seen_part):
        scores = (
            jnp.einsum("gqhd,gkhd->ghqk", query_part, key_part, preferred_element_type=jnp.float32)
            * scale_factor
        )
        return jnp.where(seen_part[:, None, None, :], scores, masked_score)

    def attend(pieces):
        query_part, key_part, value_part, seen_part = pieces
        scores = score_block(query_part, key_part, seen_part)
        highest = jnp.max(scores, axis=-1, keepdims=True)
        exp_scores = jnp.exp(scores - highest)
        totals = jnp.sum(exp_scores, axis=-1, keepdims=True)
        probs_low = (exp_scores / totals).astype(jnp.bfloat16)
        mixed_part = jnp.einsum(
            "ghqk,gkhd->gqhd", probs_low, value_part, preferred_element_type=jnp.float32
        )
        return (mixed_part.astype(jnp.bfloat16), (highest + jnp.log(totals))[..., 0])

    mixed_blk, log_totals = lax.map(attend, (query_blk, key_blk, value_blk, seen_blk))
    mixed_rows = mixed_blk.reshape(images, seq_len, half_width)
    branch = fold_rows(
        jnp.einsum("bse,ed->bsd", mixed_rows, proj_w, preferred_element_type=jnp.float32)
    )
    middle = inputs + branch + proj_b
    normed_two = spread_rows(layer_norm(middle, gain_two, bias_two).astype(jnp.bfloat16))
    hidden_pre = (
        jnp.einsum("bsd,df->bsf", normed_two, fc1_w, preferred_element_type=jnp.float32) + fc1_b
    )
    hidden = gelu_exact(hidden_pre).astype(jnp.bfloat16)
    outputs = (
        middle
        + fold_rows(jnp.einsum("bsf,fd->bsd", hidden, fc2_w, preferred_element_type=jnp.float32))
        + fc2_b
    )
    regathered = (
        lax.all_gather(ln1_gain_bf, "dp", axis=0, tiled=True),
        lax.all_gather(ln1_bias_bf, "dp", axis=0, tiled=True),
        lax.all_gather(w_qkv_bf, "dp", axis=1, tiled=True),
        lax.all_gather(qv_bias_bf, "dp", axis=1, tiled=True),
        lax.all_gather(w_proj_bf, "dp", axis=1, tiled=True),
        lax.all_gather(proj_bias_bf, "dp", axis=0, tiled=True),
        lax.all_gather(ln2_gain_bf, "dp", axis=0, tiled=True),
        lax.all_gather(ln2_bias_bf, "dp", axis=0, tiled=True),
        lax.all_gather(w_fc1_bf, "dp", axis=0, tiled=True),
        lax.all_gather(fc1_bias_bf, "dp", axis=0, tiled=True),
        lax.all_gather(w_fc2_bf, "dp", axis=1, tiled=True),
        lax.all_gather(fc2_bias_bf, "dp", axis=0, tiled=True),
    )
    backward_params = unpack(regathered, tensor_rank, half_width, half_hidden)
    (
        gain_one,
        bias_one,
        qkv_w,
        qv_b,
        proj_w,
        proj_b,
        gain_two,
        bias_two,
        fc1_w,
        fc1_b,
        fc2_w,
        fc2_b,
    ) = backward_params
    fc2_b_grad = jnp.sum(out_grad, axis=(0, 1))
    out_rows = spread_grads(out_grad.astype(jnp.bfloat16))
    fc2_w_grad = jnp.einsum("bsf,bsd->fd", hidden, out_rows, preferred_element_type=jnp.float32)
    hidden_grad = jnp.einsum("bsd,fd->bsf", out_rows, fc2_w, preferred_element_type=jnp.float32)
    gelu_back = jax.vjp(gelu_exact, hidden_pre)[1]
    pre_grad = gelu_back(hidden_grad)[0]
    fc1_b_grad = lax.dynamic_update_slice_in_dim(
        jnp.zeros((half_hidden * tensor_count,), jnp.float32),
        jnp.sum(pre_grad, axis=(0, 1)),
        tensor_rank * half_hidden,
        0,
    )
    pre_low = pre_grad.astype(jnp.bfloat16)
    fc1_w_grad = jnp.einsum("bsd,bsf->df", normed_two, pre_low, preferred_element_type=jnp.float32)
    normed_two_grad = fold_grads(
        jnp.einsum("bsf,df->bsd", pre_low, fc1_w, preferred_element_type=jnp.float32)
    )
    norm_two_back = jax.vjp(layer_norm, middle, gain_two, bias_two)[1]
    middle_part, gain_two_grad, bias_two_grad = norm_two_back(normed_two_grad)
    middle_grad = out_grad + middle_part
    proj_b_grad = jnp.sum(middle_grad, axis=(0, 1))
    middle_rows = spread_grads(middle_grad.astype(jnp.bfloat16))
    proj_w_grad = jnp.einsum(
        "bse,bsd->ed", mixed_rows, middle_rows, preferred_element_type=jnp.float32
    )
    mixed_grad = jnp.einsum(
        "bsd,ed->bse", middle_rows, proj_w, preferred_element_type=jnp.float32
    ).astype(jnp.bfloat16)
    mixed_grad_blk = by_heads(mixed_grad)

    def attend_back(pieces):
        query_part, key_part, value_part, seen_part, log_part, grad_part = pieces
        scores = score_block(query_part, key_part, seen_part)
        probs_f32 = jnp.exp(scores - log_part[..., None])
        prob_grad = jnp.einsum(
            "gqhd,gkhd->ghqk", grad_part, value_part, preferred_element_type=jnp.float32
        )
        value_grad_part = jnp.einsum(
            "ghqk,gqhd->gkhd",
            probs_f32.astype(jnp.bfloat16),
            grad_part,
            preferred_element_type=jnp.float32,
        )
        row_dot = jnp.sum(probs_f32 * prob_grad, axis=-1, keepdims=True)
        score_grad = (probs_f32 * (prob_grad - row_dot)).astype(jnp.bfloat16)
        query_grad_part = (
            jnp.einsum("ghqk,gkhd->gqhd", score_grad, key_part, preferred_element_type=jnp.float32)
            * scale_factor
        )
        key_grad_part = (
            jnp.einsum(
                "ghqk,gqhd->gkhd", score_grad, query_part, preferred_element_type=jnp.float32
            )
            * scale_factor
        )
        return (query_grad_part, key_grad_part, value_grad_part)

    query_grad, key_grad, value_grad = lax.map(
        attend_back, (query_blk, key_blk, value_blk, seen_blk, log_totals, mixed_grad_blk)
    )
    query_grad = query_grad.reshape(images, seq_len, half_width)
    key_grad = key_grad.reshape(images, seq_len, half_width)
    value_grad = value_grad.reshape(images, seq_len, half_width)
    qv_local_grad = jnp.stack([jnp.sum(query_grad, axis=(0, 1)), jnp.sum(value_grad, axis=(0, 1))])
    qv_b_grad = lax.dynamic_update_slice_in_dim(
        jnp.zeros((2, half_width * tensor_count), jnp.float32),
        qv_local_grad,
        tensor_rank * half_width,
        1,
    )
    qkv_low = jnp.stack([query_grad, key_grad, value_grad]).astype(jnp.bfloat16)
    qkv_w_grad = jnp.einsum(
        "bsd,cbse->cde", normed_one, qkv_low, preferred_element_type=jnp.float32
    )
    normed_one_grad = fold_grads(
        jnp.einsum("cbse,cde->bsd", qkv_low, qkv_w, preferred_element_type=jnp.float32)
    )
    norm_one_back = jax.vjp(layer_norm, inputs, gain_one, bias_one)[1]
    input_part, gain_one_grad, bias_one_grad = norm_one_back(normed_one_grad)
    input_grad = middle_grad + input_part
    summed = (
        lax.psum_scatter(gain_one_grad, "dp", scatter_dimension=0, tiled=True),
        lax.psum_scatter(bias_one_grad, "dp", scatter_dimension=0, tiled=True),
        lax.psum_scatter(qkv_w_grad, "dp", scatter_dimension=1, tiled=True),
        lax.psum_scatter(qv_b_grad, "dp", scatter_dimension=1, tiled=True),
        lax.psum_scatter(proj_w_grad, "dp", scatter_dimension=1, tiled=True),
        lax.psum_scatter(proj_b_grad, "dp", scatter_dimension=0, tiled=True),
        lax.psum_scatter(gain_two_grad, "dp", scatter_dimension=0, tiled=True),
        lax.psum_scatter(bias_two_grad, "dp", scatter_dimension=0, tiled=True),
        lax.psum_scatter(fc1_w_grad, "dp", scatter_dimension=0, tiled=True),
        lax.psum_scatter(fc1_b_grad, "dp", scatter_dimension=0, tiled=True),
        lax.psum_scatter(fc2_w_grad, "dp", scatter_dimension=1, tiled=True),
        lax.psum_scatter(fc2_b_grad, "dp", scatter_dimension=0, tiled=True),
    )
    vectors = lax.psum(
        (summed[0], summed[1], summed[3], summed[5], summed[6], summed[7], summed[9], summed[11]),
        "tensor",
    )
    return (
        outputs,
        input_grad,
        vectors[0],
        vectors[1],
        summed[2],
        vectors[2],
        summed[4],
        vectors[3],
        vectors[4],
        vectors[5],
        summed[8],
        vectors[6],
        summed[10],
        vectors[7],
    )


def solution(mesh):
    placed = (
        P(("dp", "tensor"), None, None),
        P("dp", None),
        P("dp"),
        P("dp"),
        P(None, "dp", "tensor"),
        P(None, "dp"),
        P("tensor", "dp"),
        P("dp"),
        P("dp"),
        P("dp"),
        P("dp", "tensor"),
        P("dp"),
        P("tensor", "dp"),
        P("dp"),
        P(("dp", "tensor"), None, None),
    )
    return jax.shard_map(
        shards,
        mesh=mesh,
        in_specs=placed,
        out_specs=(
            P(("dp", "tensor"), None, None),
            P(("dp", "tensor"), None, None),
            P("dp"),
            P("dp"),
            P(None, "dp", "tensor"),
            P(None, "dp"),
            P("tensor", "dp"),
            P("dp"),
            P("dp"),
            P("dp"),
            P("dp", "tensor"),
            P("dp"),
            P("tensor", "dp"),
            P("dp"),
        ),
        check_vma=False,
    )
```

profile of v0, /device:TPU:0, one launch (start us, length us, event | category | flops | bytes accessed | tf_op | source)
XLA Modules:
  0.0 1191.4 jit_solution(4981520248966245825)
XLA Ops:
  14.6 63.0 %all-reduce.17 = (bf16[1024]{0:T(1024)(128)(2,1)S(1)}, bf16[1024]{0:T(1024)(128)(2,1)S(1)}, bf16[1024]{0:T(1024)(128)(2,1)S(1)}, bf16[1024]{0:T(1024)(128)(2,1)S...) all-reduce(bf16[1024]{0:T(1024)(128)(2,1)S(1)} %dynamic-update-slic, ...), channel_id=1, replica_groups=mesh['dp'=16,'tensor'=2] {'dp'}, use_global_device_ids=true, to_apply=%add.2 | all-reduce | flops 6144 | bytes 24576
  84.3 17.7 %all-gather = bf16[16,64,2]{1,2,0:T(2,128)(2,1)S(1)} all-gather(bf16[1,64,2]{1,2,0:T(2,128)(2,1)S(1)} %convert_bitcast_fusion), channel_id=1, replica_groups=mesh['dp'=16,'tensor'=2] {'dp'}, dimensions={0}, use_global_device_ids=true | all-gather | bytes 4352 | tf_op jit(solution)/shard_map/all_gather | solution.py:121
  102.4 16.8 %all-gather.11.cloned.1.call-done = bf16[4,320,1024]{2,1,0:T(8,128)(2,1)} async-done(((bf16[2,320,1024]{2,1,0:T(8,128)(2,1)}), bf16[4,320,1024]{2,1,0:T(8,128)(2,1)}) %all-gather.11.cloned.1.call-update) | async-done | bytes 2621456 | tf_op jit(solution)/shard_map/all_gather | solution.py:24
  119.2 48.3 %all-gather.13.cloned.1.call-done = bf16[3,1024,512]{2,1,0:T(8,128)(2,1)} async-done(((bf16[3,64,512]{2,1,0:T(8,128)(2,1)}), bf16[3,1024,512]{2,1,0:T(8,128)(2,1)}) %all-gather.13.cloned.1.call-update) | async-done | bytes 3145744 | tf_op jit(solution)/shard_map/all_gather | solution.py:120
  167.5 6.9 fusion.67
  178.6 3.5 copy.83
  182.0 3.4 copy.81
  188.0 3.5 add_convert_fusion
  193.0 17.3 %while.26 = (s32[]{:T(128)}, bf16[2,2,320,8,64]{2,4,3,1,0:T(8,128)(2,1)}, f32[2,2,8,320]{3,2,1,0:T(8,128)S(1)}, bf16[2,2,320,8,64]{2,4,3,1,0:T(8,128)(2,1)}, pre...) while((s32[]{:T(128)}, ...), condition=%wide.region_5.6_spmd, body=%wide.region_2.5_spmd.sunk | while | flops 439413760 | bytes 29550712 | solution.py:183
  193.0 3.5 fusion.135
  198.4 3.2 fusion.137
  201.6 3.5 fusion.135
  207.0 3.2 fusion.137
  210.2 5.2 convolution_convert_fusion
  216.5 35.1 %reduce-scatter.11.cloned.1.call-done = bf16[2,320,1024]{2,1,0:T(8,128)(2,1)} async-done(((bf16[4,320,1024]{2,1,0:T(8,128)(2,1)}), bf16[2,320,1024]{2,1,0:T(8,128)(2,1)}) %reduce-scatter.11.cloned.1.call-update) | async-done | bytes 1310736 | tf_op jit(solution)/shard_map/reduce_scatter | solution.py:28
  259.4 21.5 %all-gather.1 = bf16[16,1,256]{2,1,0:T(2,128)(2,1)S(1)} all-gather(bf16[1,1,256]{2,1,0:T(2,128)(2,1)S(1)} %reshape.176), channel_id=1, replica_groups=mesh['dp'=16,'tensor'=2] {'dp'}, dimensions={0}, use_global_device_ids=true | all-gather | bytes 8704 | tf_op jit(solution)/shard_map/all_gather | solution.py:127
  281.0 23.9 %all-gather.19.cloned.1.call-done = bf16[1024,2048]{1,0:T(8,128)(2,1)} async-done(((bf16[64,2048]{1,0:T(8,128)(2,1)}), bf16[1024,2048]{1,0:T(8,128)(2,1)}) %all-gather.19.cloned.1.call-update) | async-done | bytes 4194320 | tf_op jit(solution)/shard_map/all_gather | solution.py:126
  304.9 39.5 %all-gather.17.cloned.1.call-done = bf16[4,320,1024]{2,1,0:T(8,128)(2,1)} async-done(((bf16[2,320,1024]{2,1,0:T(8,128)(2,1)}), bf16[4,320,1024]{2,1,0:T(8,128)(2,1)}) %all-gather.17.cloned.1.call-update) | async-done | bytes 2621456 | tf_op jit(solution)/shard_map/all_gather | solution.py:24
  344.4 11.8 fusion.79
  356.3 3.8 copy-done.13
  360.1 25.2 %multiply_convert_fusion.1 = (bf16[4,320,2048]{2,1,0:T(8,128)(2,1)}, f32[4,320,2048]{2,1,0:T(8,128)}) fusion(f32[4,320,2048]{2,1,0:T(8,128)S(1)} %get-tuple-element.272, f32[2048]{0:T(1024)S(1)} %dynamic_slice.40, u8[320,2048]{1,0:T(8,128)(4,1)S(1)} %get-tuple-element.185, u8[320,2048]{1,0:T(8,128)(4,1)S(1)} %get-tuple-element.184), kind=kLoop, calls=%fused_computation.64 | loop fusion | flops 186122240 | bytes 27533312 | tf_op jit(solution)/shard_map/convert_element_type | solution.py:193
  385.3 52.8 %all-gather.21.cloned.1.call-done = bf16[2048,1024]{0,1:T(8,128)(2,1)} async-done(((bf16[2048,64]{0,1:T(8,128)(2,1)}), bf16[2048,1024]{0,1:T(8,128)(2,1)}) %all-gather.21.cloned.1.call-update) | async-done | bytes 4194320 | tf_op jit(solution)/shard_map/all_gather | solution.py:128
  438.1 17.0 %fusion.106 = (f32[2048]{0:T(1024)}, bf16[4,320,2048]{2,1,0:T(8,128)(2,1)S(1)}) fusion(f32[4,320,2048]{2,1,0:T(8,128)} %get-tuple-element.254, bf16[4,320,1024]{2,1,0:T(8,128)(2,1)} %all-gather.23.cloned.1.call-done, bf16[2048,1024]{0,1:T(8,128)(2,1)} %all-gather.21.cloned.1.call-done, f32[4,320,2048]{2,1,0:T(8,128)} %copy-done.13, f32[2048]{0:T(1024)S(1)} %dynamic_slice.40), kind=kOutput, calls=%fused_computation.163 | convolution fusion | flops 5410650112 | bytes 33046528 | tf_op jit(solution)/shard_map/bsd,fd->bsf/dot_general | solution.py:231
  457.5 7.2 fusion.82
  464.8 10.1 fusion.87
  475.1 26.0 %reduce-scatter.15.cloned.1.call-done = bf16[2,320,1024]{2,1,0:T(8,128)(2,1)} async-done(((bf16[4,320,1024]{2,1,0:T(8,128)(2,1)}), bf16[2,320,1024]{2,1,0:T(8,128)(2,1)}) %reduce-scatter.15.cloned.1.call-update) | async-done | bytes 1310736 | tf_op jit(solution)/shard_map/reduce_scatter | solution.py:38
  506.0 34.9 %reduce-scatter.13.cloned.1.call-done = bf16[2,320,1024]{2,1,0:T(8,128)(2,1)} async-done(((bf16[4,320,1024]{2,1,0:T(8,128)(2,1)}), bf16[2,320,1024]{2,1,0:T(8,128)(2,1)}) %reduce-scatter.13.cloned.1.call-update) | async-done | bytes 1310736 | tf_op jit(solution)/shard_map/reduce_scatter | solution.py:28
  540.9 4.7 fusion.98
  548.5 39.1 %all-gather.25.cloned.1.call-done = bf16[4,320,1024]{2,1,0:T(8,128)(2,1)} async-done(((bf16[2,320,1024]{2,1,0:T(8,128)(2,1)}), bf16[4,320,1024]{2,1,0:T(8,128)(2,1)}) %all-gather.25.cloned.1.call-update) | async-done | bytes 2621456 | tf_op jit(solution)/shard_map/all_gather | solution.py:34
  587.6 4.7 convolution_convert_fusion.1
  595.2 28.6 %while.27 = (s32[]{:T(128)}, f32[2,2,320,8,64]{2,4,3,1,0:T(8,128)}, bf16[2,2,320,8,64]{2,4,3,1,0:T(8,128)(2,1)}, f32[2,2,320,8,64]{2,4,3,1,0:T(8,128)}, bf16[2,2...) while((s32[]{:T(128)}, f32[2,2,320,8,64]{2,4,3,1,0:T(8,128)}, ...), condition=%wide.region_15.16_spmd, body=%wide.region_13.15_spmd.sunk | while | flops 1073802240 | bytes 105150632 | solution.py:285
  597.1 3.0 multiply_reduce_fusion.4
  611.4 3.0 multiply_reduce_fusion.4
  620.8 3.0 bitcast_dynamic-update-slice_fusion.11
  623.8 5.5 fusion.102
  635.4 9.5 convolution_bitcast_fusion.2
  644.9 9.5 copy.90
  655.7 8.1 bitcast_convert_fusion
  663.9 5.6 convolution_bitcast_fusion.3
  669.8 10.4 convolution_bitcast_fusion.1
  681.9 10.4 convolution_bitcast_fusion
  695.0 169.4 %all-reduce.20.cloned.1.call-done = f32[3,1024,512]{2,0,1:T(4,128)} async-done(((f32[3,1024,512]{2,0,1:T(4,128)}), f32[3,1024,512]{2,0,1:T(4,128)}) %all-reduce.20.cloned.1.call-update) | async-done | bytes 6291472
  866.4 37.6 %reduce-scatter.17.cloned.1.call-done = bf16[2,320,1024]{2,1,0:T(8,128)(2,1)} async-done(((bf16[4,320,1024]{2,1,0:T(8,128)(2,1)}), bf16[2,320,1024]{2,1,0:T(8,128)(2,1)}) %reduce-scatter.17.cloned.1.call-update) | async-done | bytes 1310736 | tf_op jit(solution)/shard_map/reduce_scatter | solution.py:38
  907.9 61.2 %all-reduce.15 = (f32[1024]{0:T(1024)S(1)}, f32[1024]{0:T(1024)S(1)}, f32[1024]{0:T(1024)S(1)}, f32[1024]{0:T(1024)S(1)}, f32[1024]{0:T(1024)S(1)}, /*index=5*/f32[4096]{0:T(1024)S(1)}, f32[1024]{0:T(1024)S(1)}) all-reduce(f32[1024]{0:T(1024)S(1)} %get-tuple-element.188, ...), channel_id=6, replica_groups=mesh['dp'=16,'tensor'=2] {'dp'}, use_global_device_ids=true, to_apply=%region_20.21.clone | all-reduce | flops 10240 | bytes 81920
  969.5 5.5 all-reduce.16
  975.1 4.4 add_add_fusion.2
  979.5 97.5 %reduce-scatter.21.cloned.1.call-done = f32[64,2048]{1,0:T(8,128)} async-done(((f32[1024,2048]{1,0:T(8,128)}), f32[64,2048]{1,0:T(8,128)}) %reduce-scatter.21.cloned.1.call-update) | async-done | bytes 524304 | tf_op jit(solution)/shard_map/reduce_scatter | solution.py:317
  1077.0 107.6 %reduce-scatter.23.cloned.1.call-done = f32[2048,64]{0,1:T(8,128)} async-done(((f32[2048,1024]{0,1:T(8,128)}), f32[2048,64]{0,1:T(8,128)}) %reduce-scatter.23.cloned.1.call-update) | async-done | bytes 524304 | tf_op jit(solution)/shard_map/reduce_scatter | solution.py:319
  (256 shorter events, 83.8 us)
Async XLA Ops:
  7.2 72.3 %copy-start = (f32[2,320,1024]{2,1,0:T(8,128)S(1)}, f32[2,320,1024]{2,1,0:T(8,128)}, u32[]{:S(2)}) copy-start(f32[2,320,1024]{2,1,0:T(8,128)} %param.19) | copy-start | bytes 7864324
  7.2 112.0 %all-gather.11.cloned.1.call-start = ((), (), s32[]{:S(2)}) async-start(), calls=%async_computation.8 | async-start | bytes 3932160 | tf_op jit(solution)/shard_map/all_gather | solution.py:24
  77.6 5.1 copy-start.28
  80.5 3.0 copy-start.25
  81.2 3.2 copy-start.44
  81.2 21.1 %copy-start.39 = (s32[4,256]{1,0:T(4,128)S(1)}, s32[4,256]{1,0:T(4,128)}, u32[]{:S(2)}) copy-start(s32[4,256]{1,0:T(4,128)} %param.20) | copy-start | bytes 12292
  82.7 84.7 %all-gather.13.cloned.1.call-start = ((), (), s32[]{:S(2)}) async-start(), calls=%async_computation.9 | async-start | bytes 3342336 | tf_op jit(solution)/shard_map/all_gather | solution.py:120
  83.5 126.7 %all-gather.15.cloned.1.call-start = ((), (), s32[]{:S(2)}) async-start(), calls=%async_computation.10 | async-start | bytes 1114112 | tf_op jit(solution)/shard_map/all_gather | solution.py:122
  84.3 167.4 %reduce-scatter.11.cloned.1.call-start = ((), (), s32[]{:S(2)}) async-start(), calls=%async_computation.11 | async-start | bytes 3932160 | tf_op jit(solution)/shard_map/reduce_scatter | solution.py:28
  188.0 3.5 copy-start.10
  210.2 5.3 copy-start.22
  215.5 89.4 %all-gather.19.cloned.1.call-start = ((), (), s32[]{:S(2)}) async-start(), calls=%async_computation.13 | async-start | bytes 4456448 | tf_op jit(solution)/shard_map/all_gather | solution.py:126
  216.3 128.1 %all-gather.17.cloned.1.call-start = ((), (), s32[]{:S(2)}) async-start(), calls=%async_computation.12 | async-start | bytes 3932160 | tf_op jit(solution)/shard_map/all_gather | solution.py:24
  253.8 2.7 copy-start.14
  256.4 3.0 copy-start.45
  256.4 128.8 %all-gather.23.cloned.1.call-start = ((), (), s32[]{:S(2)}) async-start(), calls=%async_computation.16 | async-start | bytes 3932160 | tf_op jit(solution)/shard_map/all_gather | solution.py:34
  258.5 179.6 %all-gather.21.cloned.1.call-start = ((), (), s32[]{:S(2)}) async-start(), calls=%async_computation.14 | async-start | bytes 4456448 | tf_op jit(solution)/shard_map/all_gather | solution.py:128
  259.3 241.8 %reduce-scatter.15.cloned.1.call-start = ((), (), s32[]{:S(2)}) async-start(), calls=%async_computation.17 | async-start | bytes 3932160 | tf_op jit(solution)/shard_map/reduce_scatter | solution.py:38
  356.3 3.8 copy-start.13
  438.1 19.4 %copy-start.41 = (bf16[1024,2048]{1,0:T(8,128)(2,1)S(1)}, bf16[1024,2048]{1,0:T(8,128)(2,1)}, u32[]{:S(2)}) copy-start(bf16[1024,2048]{1,0:T(8,128)(2,1)} %all-gather.19.cloned.1.call-done) | copy-start | bytes 12582916
  455.1 2.4 copy-start.46
  464.8 76.1 %reduce-scatter.13.cloned.1.call-start = ((), (), s32[]{:S(2)}) async-start(), calls=%async_computation.15 | async-start | bytes 3932160 | tf_op jit(solution)/shard_map/reduce_scatter | solution.py:28
  464.8 10.2 copy-start.40
  475.0 26.1 %copy-start.5 = (f32[2,320,1024]{2,1,0:T(8,128)S(1)}, f32[2,320,1024]{2,1,0:T(8,128)}, u32[]{:S(2)}) copy-start(f32[2,320,1024]{2,1,0:T(8,128)} %copy-done.4) | copy-start | bytes 7864324
  475.0 112.6 %all-gather.25.cloned.1.call-start = ((), (), s32[]{:S(2)}) async-start(), calls=%async_computation.18 | async-start | bytes 3932160 | tf_op jit(solution)/shard_map/all_gather | solution.py:34
  501.1 2.9 copy-start.12
  548.4 145.7 %reduce-scatter.25.cloned.1.call-start = ((), (), s32[]{:S(2)}) async-start(), calls=%async_computation.23 | async-start | bytes 557056
  548.5 46.7 %copy-start.2 = (bf16[2,2,320,8,64]{2,4,3,1,0:T(8,128)(2,1)S(1)}, bf16[2,2,320,8,64]{2,4,3,1,0:T(8,128)(2,1)}, u32[]{:S(2)}) copy-start(bf16[2,2,320,8,64]{2,4,3,1,0:T(8,128)(2,1)} %get-tuple-element.465) | copy-start | bytes 3932164
  548.5 46.7 %copy-start.3 = (bf16[2,2,320,8,64]{2,4,3,1,0:T(8,128)(2,1)S(1)}, bf16[2,2,320,8,64]{2,4,3,1,0:T(8,128)(2,1)}, u32[]{:S(2)}) copy-start(bf16[2,2,320,8,64]{2,4,3,1,0:T(8,128)(2,1)} %get-tuple-element.466) | copy-start | bytes 3932164
  600.1 2.4 copy-start.15
  614.4 2.4 copy-start.15
  632.4 3.0 copy-start.20
  635.2 229.2 %all-reduce.20.cloned.1.call-start = ((), (), s32[]{:S(2)}) async-start(), calls=%async_computation.24 | async-start | bytes 16777216
  654.4 249.6 %reduce-scatter.17.cloned.1.call-start = ((), (), s32[]{:S(2)}) async-start(), calls=%async_computation.19 | async-start | bytes 3932160 | tf_op jit(solution)/shard_map/reduce_scatter | solution.py:38
  663.9 5.9 copy-start.42
  663.9 315.7 %reduce-scatter.19.cloned.1.call-start = ((), (), s32[]{:S(2)}) async-start(), calls=%async_computation.20 | async-start | bytes 2228224 | tf_op jit(solution)/shard_map/reduce_scatter | solution.py:313
  669.5 407.6 %reduce-scatter.21.cloned.1.call-start = ((), (), s32[]{:S(2)}) async-start(), calls=%async_computation.21 | async-start | bytes 8912896 | tf_op jit(solution)/shard_map/reduce_scatter | solution.py:317
  680.2 504.4 %reduce-scatter.23.cloned.1.call-start = ((), (), s32[]{:S(2)}) async-start(), calls=%async_computation.22 | async-start | bytes 8912896 | tf_op jit(solution)/shard_map/reduce_scatter | solution.py:319
  692.3 211.7 %copy-start.1 = (f32[2,320,1024]{2,1,0:T(8,128)S(1)}, f32[2,320,1024]{2,1,0:T(8,128)}, u32[]{:S(2)}) copy-start(f32[2,320,1024]{2,1,0:T(8,128)} %param.19) | copy-start | bytes 7864324
  692.3 211.7 %copy-start.27 = (f32[2,320]{1,0:T(2,128)S(1)}, f32[2,320]{1,0:T(2,128)}, u32[]{:S(2)}) copy-start(f32[2,320]{1,0:T(2,128)} %copy-done.26) | copy-start | bytes 7684
  692.3 211.7 %copy-start.29 = (f32[1024]{0:T(1024)S(1)}, f32[1024]{0:T(1024)}, u32[]{:S(2)}) copy-start(f32[1024]{0:T(1024)} %copy-done.28) | copy-start | bytes 12292
  692.3 214.0 %copy-start.33 = (f32[2,320]{1,0:T(2,128)S(1)}, f32[2,320]{1,0:T(2,128)}, u32[]{:S(2)}) copy-start(f32[2,320]{1,0:T(2,128)} %copy-done.32) | copy-start | bytes 7684
  692.3 214.0 %copy-start.31 = (f32[2,320]{1,0:T(2,128)S(1)}, f32[2,320]{1,0:T(2,128)}, u32[]{:S(2)}) copy-start(f32[2,320]{1,0:T(2,128)} %copy-done.30) | copy-start | bytes 7684
  866.4 41.4 %copy-start.34 = (f32[1024]{0:T(1024)S(1)}, f32[1024]{0:T(1024)}, u32[]{:S(2)}) copy-start(f32[1024]{0:T(1024)} %get-tuple-element.267) | copy-start | bytes 12292
  866.4 41.4 %copy-start.35 = (f32[1024]{0:T(1024)S(1)}, f32[1024]{0:T(1024)}, u32[]{:S(2)}) copy-start(f32[1024]{0:T(1024)} %get-tuple-element.186) | copy-start | bytes 12292
  866.4 41.4 %copy-start.36 = (f32[1024]{0:T(1024)S(1)}, f32[1024]{0:T(1024)}, u32[]{:S(2)}) copy-start(f32[1024]{0:T(1024)} %get-tuple-element.251) | copy-start | bytes 12292
  866.4 41.4 %copy-start.37 = (f32[1024]{0:T(1024)S(1)}, f32[1024]{0:T(1024)}, u32[]{:S(2)}) copy-start(f32[1024]{0:T(1024)} %get-tuple-element.190) | copy-start | bytes 12292
  904.0 2.3 copy-start.11
  (23 other events, 35.0 us)
Sparse Core Ops, SparseCore 0:
  82.8 36.2 all-gather.10
  121.9 45.4 all-gather.12
  170.2 36.1 all-gather.14
  215.6 36.0 reduce-scatter.10
  254.2 50.6 all-gather.18
  306.8 37.5 all-gather.16
  346.0 38.9 all-gather.22
  387.7 50.3 all-gather.20
  464.9 36.1 reduce-scatter.14
  503.2 37.6 reduce-scatter.12
  548.5 38.9 all-gather.24
  635.3 56.1 reduce-scatter.24
  695.3 169.0 all-reduce.19
  866.5 37.4 reduce-scatter.16
  908.2 61.9 reduce-scatter.18
  974.7 102.2 reduce-scatter.20
  1081.5 103.0 reduce-scatter.22
where the time goes:
time: 1200 us; the launch traced here: 1190 us
  waiting for transfers between devices  729 us (61%)
  blocking collectives  169 us (14%)
  matrix products  139 us (12%)
  other arithmetic  79.9 us (7%)
  local copies, waits for them, and re-layouts  56 us (5%)
  between operations  16.8 us (1%)
    unnamed x19, waiting for transfers between devices  170 us
    unnamed x2, blocking collectives  124 us
    reduce_scatter x1, waiting for transfers between devices, shards(): lax.psum_scatter(fc2_w_grad, 'dp', scatter_dimension=1, tiled=True)  108 us
    reduce_scatter x1, waiting for transfers between devices, shards(): lax.psum_scatter(fc1_w_grad, 'dp', scatter_dimension=0, tiled=True)  97.5 us
    reduce_scatter x2, waiting for transfers between devices, fold_rows(): lax.psum_scatter(values.astype(jnp.bfloat16), 'tensor', scatter_dimension...  70 us
    reduce_scatter x2, waiting for transfers between devices, fold_grads(): lax.psum_scatter(values.astype(jnp.bfloat16), 'tensor', scatter_dimension...  63.7 us
    all_gather x2, waiting for transfers between devices, spread_rows(): return lax.all_gather(values, 'tensor', axis=0, tiled=True)  56.3 us
    all_gather x1, waiting for transfers between devices, shards(): lax.all_gather(w_fc2_bf, 'dp', axis=1, tiled=True)  52.8 us
  transfers between devices with their start and end apart: 17, of which 13 were waited for; matrix products, arithmetic and copies ran while one was open for 14% of the time, Pallas kernels for 0%

commit v1 on v0

v1 whole, which is shorter than its diff:
```python
import jax
import jax.numpy as jnp
from jax import lax
from jax.experimental import pallas as pl
from jax.experimental.pallas import tpu as pltpu
from jax.sharding import PartitionSpec as P

HEAD_DIM = 64
norm_eps = 1e-06
masked_score = -1e30
AXES = ("dp", "tensor")
LOW = jnp.bfloat16
F32 = jnp.float32
TILE = 128
Y_BIT, CORE_BIT, X_BIT, Z_SHIFT = 1, 2, 4, 3
ANY = pl.BlockSpec(memory_space=pl.ANY)


def mm(left, right):
    return lax.dot_general(left, right, (((1,), (0,)), ((), ())), preferred_element_type=F32)


def mm_nt(left, right):
    return lax.dot_general(left, right, (((1,), (1,)), ((), ())), preferred_element_type=F32)


def mm_tn(left, right):
    return lax.dot_general(left, right, (((0,), (0,)), ((), ())), preferred_element_type=F32)


def whole(*shape):
    return pl.BlockSpec(shape, lambda t, me: (0,) * len(shape))


def call(body, grid, ins, outs, shapes, scratch, flops, moved, name):
    return pl.pallas_call(
        body,
        grid_spec=pltpu.PrefetchScalarGridSpec(
            num_scalar_prefetch=1,
            grid=grid,
            in_specs=ins,
            out_specs=outs,
            scratch_shapes=scratch,
        ),
        out_shape=shapes,
        compiler_params=pltpu.CompilerParams(
            dimension_semantics=("arbitrary",) * len(grid), vmem_limit_bytes=60 << 20
        ),
        cost_estimate=pl.CostEstimate(flops=flops, bytes_accessed=moved, transcendentals=0),
        name=name,
    )


def places(me, core_flip, first, second):
    owner = ((me >> 1) & 1) ^ core_flip
    off_y = jnp.where(owner == 0, first, second)
    off_x = jnp.where(owner == 0, second, first)
    return off_y, off_x


def dp_of(me, core_flip, off_x, off_z):
    core = ((me >> 1) & 1) ^ core_flip
    return (((me >> Z_SHIFT) ^ off_z) << 2) | ((((me >> 2) & 1) ^ off_x) << 1) | core


def fetch(me, pieces, store, sems, start, width):
    for index, piece in enumerate(pieces):
        core_flip, first, second = index >> 2, (index >> 1) & 1, index & 1
        off_y, off_x = places(me, core_flip, first, second)
        y_at = (me & 1) ^ off_y
        depth, rows, _ = piece.shape
        for off_z in range(depth):
            row = pl.multiple_of(dp_of(me, core_flip, off_x, off_z) * rows, rows)
            pltpu.make_async_copy(
                piece.at[off_z, :, pl.ds(start, width)],
                store.at[y_at, pl.ds(row, rows), :],
                sems.at[y_at],
            ).start()


def arrived(store, sems, y_at):
    pltpu.make_async_copy(store.at[y_at], store.at[y_at], sems.at[y_at]).wait()


def normed(rows, gain, shift):
    center = rows - jnp.mean(rows, axis=-1, keepdims=True)
    spread = jnp.mean(center * center, axis=-1, keepdims=True)
    return center * lax.rsqrt(spread + norm_eps) * gain + shift


def qkv_call(me, rows_in, table, bias, pieces):
    count, width = rows_in.shape
    half = width // 2
    span = 3 * half

    def body(me_ref, x_ref, table_ref, bias_ref, *refs):
        parts, (norm_ref, turn_ref, out_ref, store, sems) = refs[:8], refs[8:]
        step = pl.program_id(0)

        @pl.when(step == 0)
        def _():
            fetch(me_ref[0], parts, store, sems, 0, span)

            @pl.loop(0, count // TILE)
            def _(i):
                at = pl.ds(pl.multiple_of(i * TILE, TILE), TILE)
                value = normed(x_ref[at, :], table_ref[0:1, :], table_ref[1:2, :])
                norm_ref[at, :] = value.astype(LOW)
                turn_ref[:, at] = value.T.astype(LOW)

        for y_at in range(2):

            @pl.when(step == 3 * y_at)
            def _():
                arrived(store, sems, y_at)

        y_at, col = step // 3, pl.multiple_of(step % 3 * half, half)
        product = mm(norm_ref[...], store[y_at, :, pl.ds(col, half)])
        out_ref[...] = (product + bias_ref[...]).astype(LOW)

    return call(
        body,
        (6,),
        [whole(count, width), whole(*table.shape), pl.BlockSpec((1, half), lambda t, me: (0, t))]
        + [ANY] * 8,
        [
            whole(count, width),
            whole(width, count),
            pl.BlockSpec((count, half), lambda t, me: (0, t)),
        ],
        [
            jax.ShapeDtypeStruct((count, width), LOW),
            jax.ShapeDtypeStruct((width, count), LOW),
            jax.ShapeDtypeStruct((count, 2 * span), LOW),
        ],
        [pltpu.VMEM((2, width, span), LOW), pltpu.SemaphoreType.DMA((2,))],
        2 * count * width * 2 * span,
        count * width * 16 + width * span * 4,
        "qkv",
    )(me, rows_in, table, bias, *pieces)


def head_halves(shape):
    lane = lax.broadcasted_iota(jnp.int32, shape, 1)
    return lane < HEAD_DIM, lane >= HEAD_DIM


def soft(query, key, seen):
    scores = jnp.where(seen, mm_nt(query, key) * HEAD_DIM**-0.5, masked_score)
    exps = jnp.exp(scores - jnp.max(scores, axis=-1, keepdims=True))
    return exps / jnp.sum(exps, axis=-1, keepdims=True)


def attend_call(me, qkv, visible):
    images, _, seq = visible.shape
    count, full = qkv.shape
    half = full // 6

    def body(me_ref, qkv_ref, seen_ref, out_ref):
        seen = seen_ref[0] > 0

        @pl.loop(0, half // TILE)
        def _(pair):
            col = pl.multiple_of(pair * TILE, TILE)
            query = qkv_ref[:, pl.ds(col, TILE)]
            key = qkv_ref[:, pl.ds(half + col, TILE)]
            value = qkv_ref[:, pl.ds(2 * half + col, TILE)]
            lanes = head_halves(query.shape)
            mixed = []
            for keep in lanes:
                probs = soft(jnp.where(keep, query, 0), key, seen)
                mixed.append(mm(probs.astype(LOW), value))
            out_ref[:, pl.ds(col, TILE)] = jnp.where(lanes[0], mixed[0], mixed[1]).astype(LOW)

    return call(
        body,
        (images, 2),
        [
            pl.BlockSpec((seq, 3 * half), lambda i, y, me: (i, y)),
            pl.BlockSpec((1, 1, seq), lambda i, y, me: (i, 0, 0)),
        ],
        pl.BlockSpec((seq, half), lambda i, y, me: (i, y)),
        jax.ShapeDtypeStruct((count, 2 * half), LOW),
        [],
        4 * count * seq * 2 * half * 4,
        count * full * 3,
        "attend",
    )(me, qkv, visible)


def project_call(me, mixed, rows_in, table, pieces):
    count, width = rows_in.shape
    half = width // 2

    def body(me_ref, mixed_ref, x_ref, table_ref, *refs):
        parts, (mid_ref, norm_ref, turn_ref, store, sems) = refs[:8], refs[8:]
        fetch(me_ref[0], parts, store, sems, 3 * half, half)
        arrived(store, sems, 0)
        mid_ref[...] = mm_nt(mixed_ref[:, :half], store[0])
        arrived(store, sems, 1)
        mid_ref[...] += mm_nt(mixed_ref[:, half:], store[1])

        @pl.loop(0, count // TILE)
        def _(i):
            at = pl.ds(pl.multiple_of(i * TILE, TILE), TILE)
            middle = x_ref[at, :] + (mid_ref[at, :] + table_ref[4:5, :])
            mid_ref[at, :] = middle
            value = normed(middle, table_ref[5:6, :], table_ref[6:7, :])
            norm_ref[at, :] = value.astype(LOW)
            turn_ref[:, at] = value.T.astype(LOW)

    return call(
        body,
        (1,),
        [whole(count, width), whole(count, width), whole(*table.shape)] + [ANY] * 8,
        [whole(count, width), whole(count, width), whole(width, count)],
        [
            jax.ShapeDtypeStruct((count, width), F32),
            jax.ShapeDtypeStruct((count, width), LOW),
            jax.ShapeDtypeStruct((width, count), LOW),
        ],
        [pltpu.VMEM((2, width, half), LOW), pltpu.SemaphoreType.DMA((2,))],
        2 * count * width * width,
        count * width * 14 + width * width * 2,
        "project",
    )(me, mixed, rows_in, table, *pieces)


def expand_call(me, normed_two, bias, pieces):
    count, width = normed_two.shape
    span = bias.shape[1] // 2
    chunk = span // 4

    def body(me_ref, norm_ref, bias_ref, *refs):
        parts, (hid_ref, slope_ref, store, sems) = refs[:8], refs[8:]
        step = pl.program_id(0)

        @pl.when(step == 0)
        def _():
            fetch(me_ref[0], parts, store, sems, 0, span)

        for y_at in range(2):

            @pl.when(step == 4 * y_at)
            def _():
                arrived(store, sems, y_at)

        y_at, col = step // 4, pl.multiple_of(step % 4 * chunk, chunk)
        pre = mm(norm_ref[...], store[y_at, :, pl.ds(col, chunk)]) + bias_ref[...]
        below = 0.5 + 0.5 * lax.erf(pre * 0.5**0.5)
        hid_ref[...] = (pre * below).astype(LOW)
        slope_ref[...] = (below + pre * jnp.exp(pre * pre * -0.5) * 0.3989422804014327).astype(LOW)

    out = pl.BlockSpec((count, chunk), lambda t, me: (0, t))
    return call(
        body,
        (8,),
        [whole(count, width), pl.BlockSpec((1, chunk), lambda t, me: (0, t))] + [ANY] * 8,
        [out, out],
        [jax.ShapeDtypeStruct((count, 2 * span), LOW)] * 2,
        [pltpu.VMEM((2, width, span), LOW), pltpu.SemaphoreType.DMA((2,))],
        2 * count * width * 2 * span,
        count * span * 8 + width * span * 4,
        "expand",
    )(me, normed_two, bias, *pieces)


def contract_call(me, hidden, slope, out_low, middle, table, pieces):
    count, width = middle.shape
    span = hidden.shape[1] // 2
    chunk = span // 4

    def body(me_ref, hid_ref, slope_ref, low_ref, mid_ref, table_ref, *refs):
        parts, (act_ref, pre_ref, sum_ref, store, sems) = refs[:8], refs[8:]
        step = pl.program_id(0)

        @pl.when(step == 0)
        def _():
            fetch(me_ref[0], parts, store, sems, 0, span)
            act_ref[...] = mid_ref[...] + table_ref[7:8, :]

        for y_at in range(2):

            @pl.when(step == 4 * y_at)
            def _():
                arrived(store, sems, y_at)

        y_at, col = step // 4, pl.multiple_of(step % 4 * chunk, chunk)
        weight = store[y_at, :, pl.ds(col, chunk)]
        act_ref[...] += mm_nt(hid_ref[...], weight)
        pre = mm(low_ref[...], weight) * slope_ref[...].astype(F32)
        pre_ref[...] = pre.astype(LOW)
        sum_ref[...] = jnp.sum(pre, axis=0, keepdims=True)

    part = pl.BlockSpec((count, chunk), lambda t, me: (0, t))
    return call(
        body,
        (8,),
        [part, part, whole(count, width), whole(count, width), whole(*table.shape)] + [ANY] * 8,
        [whole(count, width), part, pl.BlockSpec((1, chunk), lambda t, me: (0, t))],
        [
            jax.ShapeDtypeStruct((count, width), F32),
            jax.ShapeDtypeStruct((count, 2 * span), LOW),
            jax.ShapeDtypeStruct((1, 2 * span), F32),
        ],
        [pltpu.VMEM((2, width, span), LOW), pltpu.SemaphoreType.DMA((2,))],
        4 * count * width * 2 * span,
        count * span * 12 + width * span * 4,
        "contract",
    )(me, hidden, slope, out_low, middle, table, *pieces)


def norm_back_call(me, low, start, gain_row, rows_in, base, table, pieces, keep_low, name):
    count, width = rows_in.shape
    span = low.shape[1] // 2
    chunk = span // 2

    def body(me_ref, low_ref, x_ref, base_ref, table_ref, *refs):
        parts, outs = refs[:8], refs[8:]
        if keep_low:
            grad_ref, vec_ref, out_low_ref, turn_ref, store, sems = outs
        else:
            grad_ref, vec_ref, store, sems = outs
        step = pl.program_id(0)

        @pl.when(step == 0)
        def _():
            fetch(me_ref[0], parts, store, sems, start, span)

        for y_at in range(2):

            @pl.when(step == 2 * y_at)
            def _():
                arrived(store, sems, y_at)

        y_at, col = step // 2, pl.multiple_of(step % 2 * chunk, chunk)
        product = mm_nt(low_ref[...], store[y_at, :, pl.ds(col, chunk)])

        @pl.when(step == 0)
        def _():
            grad_ref[...] = product

        @pl.when(step > 0)
        def _():
            grad_ref[...] += product

        @pl.when(step == 3)
        def _():
            vec_ref[...] = jnp.zeros_like(vec_ref)

            @pl.loop(0, count // TILE)
            def _(i):
                at = pl.ds(pl.multiple_of(i * TILE, TILE), TILE)
                back = grad_ref[at, :]
                rows = x_ref[at, :]
                center = rows - jnp.mean(rows, axis=-1, keepdims=True)
                spread = jnp.mean(center * center, axis=-1, keepdims=True)
                scale = lax.rsqrt(spread + norm_eps)
                unit = center * scale
                inner = back * table_ref[gain_row : gain_row + 1, :]
                along = jnp.mean(inner * unit, axis=-1, keepdims=True)
                level = jnp.mean(inner, axis=-1, keepdims=True)
                grad = base_ref[at, :] + scale * (inner - level - unit * along)
                grad_ref[at, :] = grad
                vec_ref[0:1, :] += jnp.sum(back * unit, axis=0, keepdims=True)
                vec_ref[1:2, :] += jnp.sum(back, axis=0, keepdims=True)
                vec_ref[2:3, :] += jnp.sum(grad, axis=0, keepdims=True)
                if keep_low:
                    out_low_ref[at, :] = grad.astype(LOW)
                    turn_ref[:, at] = grad.T.astype(LOW)

    outs = [whole(count, width), whole(8, width)]
    shapes = [jax.ShapeDtypeStruct((count, width), F32), jax.ShapeDtypeStruct((8, width), F32)]
    if keep_low:
        outs += [whole(count, width), whole(width, count)]
        shapes += [
            jax.ShapeDtypeStruct((count, width), LOW),
            jax.ShapeDtypeStruct((width, count), LOW),
        ]
    return call(
        body,
        (4,),
        [
            pl.BlockSpec((count, chunk), lambda t, me: (0, t)),
            whole(count, width),
            whole(count, width),
            whole(*table.shape),
        ]
        + [ANY] * 8,
        outs,
        shapes,
        [pltpu.VMEM((2, width, span), LOW), pltpu.SemaphoreType.DMA((2,))],
        2 * count * width * 2 * span,
        count * width * 16 + width * span * 4 + count * span * 4,
        name,
    )(me, low, rows_in, base, table, *pieces)


def mixed_back_call(me, middle_low, pieces):
    count, width = middle_low.shape
    half = width // 2

    def body(me_ref, low_ref, *refs):
        parts, (out_ref, store, sems) = refs[:8], refs[8:]
        step = pl.program_id(0)

        @pl.when(step == 0)
        def _():
            fetch(me_ref[0], parts, store, sems, 3 * half, half)

        for y_at in range(2):

            @pl.when(step == y_at)
            def _():
                arrived(store, sems, y_at)

        out_ref[...] = mm(low_ref[...], store[step]).astype(LOW)

    return call(
        body,
        (2,),
        [whole(count, width)] + [ANY] * 8,
        pl.BlockSpec((count, half), lambda t, me: (0, t)),
        jax.ShapeDtypeStruct((count, width), LOW),
        [pltpu.VMEM((2, width, half), LOW), pltpu.SemaphoreType.DMA((2,))],
        2 * count * width * width,
        count * width * 4 + width * width * 2,
        "mixed_back",
    )(me, middle_low, *pieces)


def attend_back_call(me, qkv, grads, visible):
    images, _, seq = visible.shape
    count, full = qkv.shape
    half = full // 6
    scale = HEAD_DIM**-0.5

    def body(me_ref, qkv_ref, grad_ref, seen_ref, out_ref, sum_ref):
        seen = seen_ref[0] > 0

        @pl.loop(0, half // TILE)
        def _(pair):
            col = pl.multiple_of(pair * TILE, TILE)
            query = qkv_ref[:, pl.ds(col, TILE)]
            key = qkv_ref[:, pl.ds(half + col, TILE)]
            value = qkv_ref[:, pl.ds(2 * half + col, TILE)]
            grad = grad_ref[:, pl.ds(col, TILE)]
            lanes = head_halves(query.shape)
            parts = []
            for keep in lanes:
                probs = soft(jnp.where(keep, query, 0), key, seen)
                prob_grad = mm_nt(jnp.where(keep, grad, 0), value)
                row_dot = jnp.sum(probs * prob_grad, axis=-1, keepdims=True)
                score_grad = (probs * (prob_grad - row_dot)).astype(LOW)
                parts.append(
                    (
                        mm(score_grad, key) * scale,
                        mm_tn(score_grad, query) * scale,
                        mm_tn(probs.astype(LOW), grad),
                    )
                )
            for at in range(3):
                merged = jnp.where(lanes[0], parts[0][at], parts[1][at])
                out_ref[:, pl.ds(at * half + col, TILE)] = merged.astype(LOW)
                sum_ref[0, 0, :, pl.ds(at * half + col, TILE)] = jnp.sum(
                    merged, axis=0, keepdims=True
                )

    return call(
        body,
        (images, 2),
        [
            pl.BlockSpec((seq, 3 * half), lambda i, y, me: (i, y)),
            pl.BlockSpec((seq, half), lambda i, y, me: (i, y)),
            pl.BlockSpec((1, 1, seq), lambda i, y, me: (i, 0, 0)),
        ],
        [
            pl.BlockSpec((seq, 3 * half), lambda i, y, me: (i, y)),
            pl.BlockSpec((1, 1, 1, 3 * half), lambda i, y, me: (i, y, 0, 0)),
        ],
        [
            jax.ShapeDtypeStruct((count, full), LOW),
            jax.ShapeDtypeStruct((images, 2, 1, 3 * half), F32),
        ],
        [],
        10 * count * seq * 2 * half * 4,
        count * full * 5,
        "attend_back",
    )(me, qkv, grads, visible)


def weight_grad_call(me, turned, right, depth, core_flip, received, name):
    width, count = turned.shape
    span = right.shape[1] // 2
    chunk = next(c for c in (1024, 768, 512, 384, 256, 128) if span % c == 0)
    parts = span // chunk
    rows = width // (4 * depth)

    def spot(t):
        first = 1 - t // (2 * parts)
        return first, t // parts % 2, t % parts

    def right_at(t, me):
        first, second, part = spot(t)
        off_y, _ = places(me[0], core_flip, first, second)
        return 0, ((me[0] & 1) ^ off_y) * parts + part

    def body(me_ref, turn_ref, right_ref, *refs):
        step = pl.program_id(0)
        first, second, _ = spot(step)
        _, off_x = places(me_ref[0], core_flip, first, second)
        lefts = refs[-1]
        for off_z in range(depth):
            row = pl.multiple_of(dp_of(me_ref[0], core_flip, off_x, off_z) * rows, rows)
            lefts[off_z * rows : (off_z + 1) * rows, :] = turn_ref[pl.ds(row, rows), :]
        product = mm(lefts[...], right_ref[...])
        if core_flip:
            refs[0][0, 0] = product.astype(LOW).reshape(depth, rows, chunk)
            return
        total = product.reshape(depth, rows, chunk) + refs[0][0, 0].astype(F32)
        for at in range(2):

            @pl.when(first == at)
            def _():
                refs[1 + at][0] = total.astype(LOW)

    def both(t, me):
        first, second, part = spot(t)
        return first, second, 0, 0, part

    def only(at):
        def index(t, me):
            first, second, part = spot(t)
            idle_second, idle_part = (0, 0) if at == 0 else (1, parts - 1)
            return (
                jnp.where(first == at, second, idle_second),
                0,
                0,
                jnp.where(first == at, part, idle_part),
            )

        return index

    block5 = pl.BlockSpec((1, 1, depth, rows, chunk), both)
    ins = [whole(width, count), pl.BlockSpec((count, chunk), right_at)]
    if core_flip:
        outs = block5
        shapes = jax.ShapeDtypeStruct((2, 2, depth, rows, span), LOW)
        extra = ()
    else:
        ins = ins + [block5]
        outs = [pl.BlockSpec((1, depth, rows, chunk), only(at)) for at in range(2)]
        shapes = [jax.ShapeDtypeStruct((2, depth, rows, span), LOW)] * 2
        extra = (received,)
    return call(
        body,
        (4 * parts,),
        ins,
        outs,
        shapes,
        [pltpu.VMEM((width // 4, count), LOW)],
        2 * count * width * span,
        count * (width + span * 2) * 2 + width * span * 4,
        name,
    )(me, turned, right, *extra)


def swap(value, size, bits, other=None):
    other = bits if other is None else other
    return lax.ppermute(
        value, AXES, [(i, i ^ (other if i & CORE_BIT else bits)) for i in range(size)]
    )


def gather_pieces(piece, size, depth):
    own = jnp.stack([piece] + [swap(piece, size, k << Z_SHIFT) for k in range(1, depth)])
    first = swap(own, size, Y_BIT, X_BIT)
    second = swap(own, size, X_BIT, Y_BIT)
    both = swap(first, size, X_BIT, Y_BIT)
    held = [own, second, first, both]
    return held + [swap(value, size, CORE_BIT) for value in held]


def gather_vectors(vector, size, depth, dp_rank):
    dp_size = 4 * depth
    held = jnp.stack([vector] + [swap(vector, size, k << Z_SHIFT) for k in range(1, depth)])
    held = jnp.stack([held, swap(held, size, X_BIT)], axis=1)
    held = jnp.stack([held, swap(held, size, CORE_BIT)], axis=2)
    held = held.reshape(dp_size, -1)
    spot = jnp.arange(dp_size)
    pick = (spot[None, :] == (spot ^ dp_rank)[:, None]).astype(F32)
    return jnp.matmul(pick, held, precision=lax.Precision.HIGHEST)


def finish_scatter(kept, sent, size, depth):
    received = swap(sent, size, Y_BIT, X_BIT)
    total = (kept.astype(F32) + received.astype(F32)).astype(LOW)
    received = swap(total[1], size, X_BIT, Y_BIT)
    total = (total[0].astype(F32) + received.astype(F32)).astype(LOW)
    result = total[0].astype(F32)
    for k in range(1, depth):
        result = result + swap(total[k], size, k << Z_SHIFT).astype(F32)
    return result


def sum_all(value, size, depth):
    for bits in (CORE_BIT, X_BIT, Y_BIT):
        value = value + swap(value, size, bits)
    return sum((swap(value, size, k << Z_SHIFT) for k in range(1, depth)), value)


def shards(
    inputs,
    key_mask,
    ln1_gain,
    ln1_bias,
    w_qkv,
    qv_bias,
    w_proj,
    proj_bias,
    ln2_gain,
    ln2_bias,
    w_fc1,
    fc1_bias,
    w_fc2,
    fc2_bias,
    out_grad,
):
    tensor_rank = lax.axis_index("tensor")
    dp_rank = lax.axis_index("dp")
    dp_size = lax.axis_size("dp")
    size = 2 * dp_size
    depth = dp_size // 4
    own_images, seq, width = inputs.shape
    count = own_images * seq
    half = w_qkv.shape[2]
    rows = ln1_gain.shape[0]
    me = jnp.reshape(dp_rank * 2 + tensor_rank, (1,)).astype(jnp.int32)

    piece_one = jnp.concatenate([w_qkv[0], w_qkv[1], w_qkv[2], w_proj.T], axis=1).astype(LOW)
    piece_two = w_fc1.astype(LOW)
    piece_three = w_fc2.T.astype(LOW)
    vector = jnp.concatenate(
        [
            ln1_gain,
            ln1_bias,
            qv_bias[0],
            qv_bias[1],
            proj_bias,
            ln2_gain,
            ln2_bias,
            fc2_bias,
            fc1_bias,
        ]
    )
    vector = jnp.pad(vector.astype(LOW).astype(F32), (0, -vector.shape[0] % 1024))
    pieces_one = gather_pieces(piece_one, size, depth)
    gathered = gather_vectors(vector.reshape(-1, TILE), size, depth, dp_rank)
    pieces_two = gather_pieces(piece_two, size, depth)
    pieces_three = gather_pieces(piece_three, size, depth)
    table = gathered[:, : 8 * rows].reshape(dp_size, 8, rows).transpose(1, 0, 2).reshape(8, width)
    fc1_full = gathered[:, 8 * rows : 12 * rows].reshape(1, 4 * width)
    qkv_bias = jnp.stack(
        [table[2].reshape(2, half), jnp.zeros((2, half), F32), table[3].reshape(2, half)], axis=1
    ).reshape(1, 6 * half)

    rows_in = inputs.reshape(count, width)
    grad_in = out_grad.reshape(count, width)
    out_low = grad_in.astype(LOW)
    out_turned = out_low.T
    own_mask = lax.dynamic_slice_in_dim(key_mask, tensor_rank * own_images, own_images, 0)
    visible = jnp.concatenate(
        [jnp.ones((own_images, seq - key_mask.shape[1]), jnp.int32), own_mask], axis=1
    )[:, None, :]

    normed_one, turned_one, qkv = qkv_call(me, rows_in, table, qkv_bias, pieces_one)
    mixed = attend_call(me, qkv, visible)
    middle, normed_two, turned_two = project_call(me, mixed, rows_in, table, pieces_one)
    hidden, slope = expand_call(me, normed_two, fc1_full, pieces_two)

    def weight_grad(turned, right, name):
        sent = weight_grad_call(me, turned, right, depth, 1, None, name + "_far")
        received = swap(sent, size, CORE_BIT)
        kept, sent = weight_grad_call(me, turned, right, depth, 0, received, name + "_near")
        return finish_scatter(kept, sent, size, depth)

    fc2_grad = weight_grad(out_turned, hidden, "fc2_grad")
    outputs, pre_low, fc1_sum = contract_call(
        me, hidden, slope, out_low, middle, table, pieces_three
    )
    fc1_grad = weight_grad(turned_two, pre_low, "fc1_grad")
    middle_grad, vec_two, middle_low, turned_mid = norm_back_call(
        me, pre_low, 0, 5, middle, grad_in, table, pieces_two, True, "norm_two_back"
    )
    proj_grad = weight_grad(turned_mid, mixed, "proj_grad")
    mixed_grad = mixed_back_call(me, middle_low, pieces_one)
    qkv_low, qkv_sum = attend_back_call(me, qkv, mixed_grad, visible)
    qkv_grad = weight_grad(turned_one, qkv_low, "qkv_grad")
    input_grad, vec_one = norm_back_call(
        me, qkv_low, 0, 0, rows_in, middle_grad, table, pieces_one, False, "norm_one_back"
    )

    qkv_sum = jnp.sum(qkv_sum, axis=(0, 2)).reshape(2, 3, half)
    sums = jnp.concatenate(
        [
            vec_one[:2],
            qkv_sum[:, 0].reshape(1, width),
            qkv_sum[:, 2].reshape(1, width),
            vec_two[2:3],
            vec_two[:2],
            jnp.sum(grad_in, axis=0, keepdims=True),
            fc1_sum.reshape(4, width),
        ]
    )
    sums = sum_all(sums, size, depth)
    mine = lax.dynamic_slice_in_dim(sums[:8], dp_rank * rows, rows, 1)
    fc1_mine = lax.dynamic_slice_in_dim(sums[8:].reshape(-1), dp_rank * 4 * rows, 4 * rows, 0)
    return (
        outputs.reshape(inputs.shape),
        input_grad.reshape(inputs.shape),
        mine[0],
        mine[1],
        qkv_grad.reshape(rows, 3, half).transpose(1, 0, 2),
        mine[2:4],
        proj_grad.T,
        mine[4],
        mine[5],
        mine[6],
        fc1_grad,
        fc1_mine,
        fc2_grad.T,
        mine[7],
    )


def solution(mesh):
    placed = (
        P(("dp", "tensor"), None, None),
        P("dp", None),
        P("dp"),
        P("dp"),
        P(None, "dp", "tensor"),
        P(None, "dp"),
        P("tensor", "dp"),
        P("dp"),
        P("dp"),
        P("dp"),
        P("dp", "tensor"),
        P("dp"),
        P("tensor", "dp"),
        P("dp"),
        P(("dp", "tensor"), None, None),
    )
    return jax.shard_map(
        shards,
        mesh=mesh,
        in_specs=placed,
        out_specs=(
            P(("dp", "tensor"), None, None),
            P(("dp", "tensor"), None, None),
            P("dp"),
            P("dp"),
            P(None, "dp", "tensor"),
            P(None, "dp"),
            P("tensor", "dp"),
            P("dp"),
            P("dp"),
            P("dp"),
            P("dp", "tensor"),
            P("dp"),
            P("tensor", "dp"),
            P("dp"),
        ),
        check_vma=False,
    )
```

time: 1200 us -> 527 us (0.44)
  waiting for transfers between devices: 729 us -> 184 us
  Pallas kernels: 0 us -> 214 us
  blocking collectives: 169 us -> 0 us
  matrix products: 139 us -> 0.22 us
  starting transfers between devices: 1.26 us -> 81.8 us
  other arithmetic: 79.9 us -> 21.7 us
  local copies, waits for them, and re-layouts: 56 us -> 21.1 us
  between operations: 16.8 us -> 1.28 us
    reduce_scatter x7 -> x0, waiting for transfers between devices: 339 us -> none  [the longest x1 108 us: shards(): lax.psum_scatter(fc2_w_grad, 'dp', scatter_dimension=1, tiled=True)]
    all_gather x8 -> x0, waiting for transfers between devices: 220 us -> none  [the longest x2 56.3 us: spread_rows(): return lax.all_gather(values, 'tensor', axis=0, tiled=True)]
    pallas_call x0 -> x17, Pallas kernels: none -> 214 us  [the longest x8 73.2 us: weight_grad_call(): call(body, (4 * parts,), ins, outs, shapes, [pltpu.VMEM((width // 4, coun...]
    ppermute x0 -> x65, waiting for transfers between devices: none -> 184 us  [swap(): lax.ppermute(value, AXES, [(i, i ^ (other if i & CORE_BIT else bits)) for...]
    unnamed x19 -> x0, waiting for transfers between devices: 170 us -> none
    dot_general x26 -> x1, matrix products: 139 us -> 0.22 us  [gather_vectors(): return jnp.matmul(pick, held, precision=lax.Precision.HIGHEST)]
    unnamed x2 -> x0, blocking collectives: 124 us -> none
    ppermute x0 -> x65, starting transfers between devices: none -> 81.8 us  [swap(): lax.ppermute(value, AXES, [(i, i ^ (other if i & CORE_BIT else bits)) for...]
  transfers between devices with their start and end apart: 17 -> 65, of which waited for: 13 -> 25; matrix products, arithmetic and copies ran while one was open for 14% -> 7% of each run, Pallas kernels for 0% -> 25%
where the time goes in v1:
time: 527 us; the launch traced here: 524 us
  Pallas kernels  214 us (41%)
  waiting for transfers between devices  184 us (35%)
  starting transfers between devices  81.8 us (16%)
  other arithmetic  21.7 us (4%)
  local copies, waits for them, and re-layouts  21.1 us (4%)
    ppermute x65, waiting for transfers between devices, swap(): lax.ppermute(value, AXES, [(i, i ^ (other if i & CORE_BIT else bits)) for...  184 us
    ppermute x65, starting transfers between devices, swap(): lax.ppermute(value, AXES, [(i, i ^ (other if i & CORE_BIT else bits)) for...  81.8 us
    pallas_call x8, Pallas kernels, weight_grad_call(): call(body, (4 * parts,), ins, outs, shapes, [pltpu.VMEM((width // 4, coun...  73.2 us
    pallas_call x2, Pallas kernels, norm_back_call(): call(body, (4,), [pl.BlockSpec((count, chunk), lambda t, me: (0, t)), who...  33.6 us
    pallas_call x1, Pallas kernels, attend_back_call(): call(body, (images, 2), [pl.BlockSpec((seq, 3 * half), lambda i, y, me: (...  27.6 us
    pallas_call x1, Pallas kernels, contract_call(): call(body, (8,), [part, part, whole(count, width), whole(count, width), w...  20 us
    pallas_call x1, Pallas kernels, attend_call(): call(body, (images, 2), [pl.BlockSpec((seq, 3 * half), lambda i, y, me: (...  18.3 us
    pallas_call x1, Pallas kernels, expand_call(): call(body, (8,), [whole(count, width), pl.BlockSpec((1, chunk), lambda t,...  16.2 us
  transfers between devices with their start and end apart: 65, of which 25 were waited for; matrix products, arithmetic and copies ran while one was open for 7% of the time, Pallas kernels for 25%

profile of v1, /device:TPU:0, one launch (start us, length us, event | category | flops | bytes accessed | tf_op | source)
XLA Modules:
  0.0 524.2 jit_solution(6636327910590722331)
XLA Ops:
  2.8 3.1 collective-permute-start.5
  5.9 2.6 collective-permute-start.6
  14.8 3.5 collective-permute-start.1
  18.3 4.6 collective-permute-done
  22.8 2.5 collective-permute-start.2
  25.3 6.4 %collective-permute-done.1 = f32[8,128]{1,0:T(8,128)S(1)} collective-permute-done((f32[8,128]{1,0:T(8,128)S(1)}, f32[8,128]{1,0:T(8,128)S(1)}, u32[]{:S(2)}, u32[]{:S(2)}) %collective-permute-start.1) | collective-permute-done | bytes 4128 | tf_op jit(solution)/shard_map/ppermute | solution.py:570
  35.5 1.9 collective-permute-start.16
  40.9 5.6 %collective-permute-done.15 = bf16[64,2048]{1,0:T(8,128)(2,1)S(1)} collective-permute-done((bf16[64,2048]{1,0:T(8,128)(2,1)S(1)}, bf16[64,2048]{1,0:T(8,128)(2,1)S(1)}, u32[]{:S(2)}, u32[]{:S(2)}) %collective-permute-start.15) | collective-permute-done | bytes 262176 | tf_op jit(solution)/shard_map/ppermute | solution.py:570
  47.1 9.6 %collective-permute-done.16 = bf16[64,2048]{1,0:T(8,128)(2,1)S(1)} collective-permute-done((bf16[64,2048]{1,0:T(8,128)(2,1)S(1)}, bf16[64,2048]{1,0:T(8,128)(2,1)S(1)}, u32[]{:S(2)}, u32[]{:S(2)}) %collective-permute-start.16) | collective-permute-done | bytes 262176 | tf_op jit(solution)/shard_map/ppermute | solution.py:570
  56.8 2.5 collective-permute-start.27
  61.0 17.8 %collective-permute-done.26 = bf16[64,2048]{1,0:T(8,128)(2,1)S(1)} collective-permute-done((bf16[64,2048]{1,0:T(8,128)(2,1)S(1)}, bf16[64,2048]{1,0:T(8,128)(2,1)S(1)}, u32[]{:S(2)}, u32[]{:S(2)}) %collective-permute-start.26) | collective-permute-done | bytes 262176 | tf_op jit(solution)/shard_map/ppermute | solution.py:570
  84.2 20.7 %collective-permute-done.19.refs_2_ = bf16[4,64,2048]{2,1,0:T(8,128)(2,1)} collective-permute-done((bf16[4,64,2048]{2,1,0:T(8,128)(2,1)S(1)}, bf16[4,64,2048]{2,1,0:T(8,128)(2,1)}, u32[]{:S(2)}, u32[]{:S(2)}) %collective-permute-start.19) | collective-permute-done | bytes 1048608 | tf_op jit(solution)/shard_map/ppermute | solution.py:570
  107.5 19.8 %collective-permute-done.29.refs_2_ = bf16[4,64,2048]{2,1,0:T(8,128)(2,1)S(1)} collective-permute-done((bf16[4,64,2048]{2,1,0:T(8,128)(2,1)}, bf16[4,64,2048]{2,1,0:T(8,128)(2,1)S(1)}, u32[]{:S(2)}, u32[]{:S(2)}) %collective-permute-start.29) | collective-permute-done | bytes 1048608 | tf_op jit(solution)/shard_map/ppermute | solution.py:570
  129.5 2.1 collective-permute-done.10.refs_3_
  134.6 2.0 copy.39
  138.8 4.7 collective-permute-done.20.refs_3_
  146.4 8.3 %collective-permute-done.30.refs_3_ = bf16[4,64,2048]{2,1,0:T(8,128)(2,1)} collective-permute-done((bf16[4,64,2048]{2,1,0:T(8,128)(2,1)}, bf16[4,64,2048]{2,1,0:T(8,128)(2,1)}, u32[]{:S(2)}, u32[]{:S(2)}) %collective-permute-start.30) | collective-permute-done | bytes 1048608 | tf_op jit(solution)/shard_map/ppermute | solution.py:570
  155.2 10.8 %qkv.1 = (bf16[640,1024]{1,0:T(8,128)(2,1)}, bf16[1024,640]{1,0:T(8,128)(2,1)}, bf16[640,3072]{1,0:T(8,128)(2,1)}) custom-call(s32[1]{0:T(128)} %bitcast.me_ref, f32[640,1024]{1,0:T(8,128)} %bitcast.172, f32[8,1024]{1,0:T(8,128)} %reshape.152.table_ref, f32[1,3072]{1,0:T(1,128)} %reshape.153.bias_ref, bf16[4,64,2048]{2,1,0:T(8,128)(2,1)} %copy-done.3, ...), custom_call_target="tpu_custom_call" | custom-call | flops 4026531840 | bytes 16777216 | tf_op jit(solution)/shard_map/qkv/pallas_call | solution.py:121
  166.1 18.3 %attend.1.mixed_ref.right_ref = bf16[640,1024]{1,0:T(8,128)(2,1)} custom-call(s32[1]{0:T(128)} %bitcast.me_ref, bf16[640,3072]{1,0:T(8,128)(2,1)} %get-tuple-element.40.qkv_ref, s32[2,1,320]{2,1,0:T(1,128)} %broadcast_in_dim.4.seen_ref), custom_call_target="tpu_custom_call" | custom-call | flops 3355443200 | bytes 5898240 | tf_op jit(solution)/shard_map/attend/pallas_call | solution.py:175
  184.4 9.2 %project.1 = (f32[640,1024]{1,0:T(8,128)}, bf16[640,1024]{1,0:T(8,128)(2,1)}, bf16[1024,640]{1,0:T(8,128)(2,1)}) custom-call(s32[1]{0:T(128)} %bitcast.me_ref, bf16[640,1024]{1,0:T(8,128)(2,1)} %attend.1.mixed_ref.right_ref, f32[640,1024]{1,0:T(8,128)} %bitcast.173, f32[8,1024]{1,0:T(8,128)} %reshape.152.table_ref, bf16[4,64,2048]{2,1,0:T(8,128)(2,1)} %copy-done.3, ...), custom_call_target="tpu_custom_call" | custom-call | flops 1342177280 | bytes 11272192 | tf_op jit(solution)/shard_map/project/pallas_call | solution.py:212
  194.6 16.2 %expand.1 = (bf16[640,4096]{1,0:T(8,128)(2,1)}, bf16[640,4096]{1,0:T(8,128)(2,1)}) custom-call(s32[1]{0:T(128)} %bitcast.me_ref, bf16[640,1024]{1,0:T(8,128)(2,1)} %get-tuple-element.41.norm_ref, f32[1,4096]{1,0:T(1,128)} %bitcast.197, bf16[4,64,2048]{2,1,0:T(8,128)(2,1)} %copy-done.14, bf16[4,64,2048]{2,1,0:T(8,128)(2,1)} %collective-permute-done.18.refs_1_, ...), custom_call_target="tpu_custom_call" | custom-call | flops 5368709120 | bytes 18874368 | tf_op jit(solution)/shard_map/expand/pallas_call | solution.py:255
  210.8 20.0 %contract.1 = (f32[640,1024]{1,0:T(8,128)}, bf16[640,4096]{1,0:T(8,128)(2,1)}, f32[1,4096]{1,0:T(1,128)}) custom-call(s32[1]{0:T(128)} %bitcast.me_ref, bf16[640,4096]{1,0:T(8,128)(2,1)} %get-tuple-element.42.hid_ref.right_ref, bf16[640,4096]{1,0:T(8,128)(2,1)} %get-tuple-element.43.slope_ref, bf16[640,1024]{1,0:T(8,128)(2,1)} %copy.40.low_ref, ...), custom_call_target="tpu_custom_call" | custom-call | flops 10737418240 | bytes 24117248 | tf_op jit(solution)/shard_map/contract/pallas_call | solution.py:296
  230.8 18.4 %norm_two_back.1 = (f32[640,1024]{1,0:T(8,128)}, f32[8,1024]{1,0:T(8,128)}, bf16[640,1024]{1,0:T(8,128)(2,1)}, bf16[1024,640]{1,0:T(8,128)(2,1)}) custom-call(s32[1]{0:T(128)} %bitcast.me_ref, bf16[640,4096]{1,0:T(8,128)(2,1)} %get-tuple-element.46.low_ref.right_ref, f32[640,1024]{1,0:T(8,128)} %get-tuple-element.44.mid_ref.x_ref, f32[640,1024]{1,0:T(8,128)} %bitcast.171, ...), custom_call_target="tpu_custom_call" | custom-call | flops 5368709120 | bytes 24117248 | tf_op jit(solution)/shard_map/norm_two_back/pallas_call | solution.py:380
  249.2 5.4 %mixed_back.1.grad_ref = bf16[640,1024]{1,0:T(8,128)(2,1)} custom-call(s32[1]{0:T(128)} %bitcast.me_ref, bf16[640,1024]{1,0:T(8,128)(2,1)} %get-tuple-element.47.low_ref, bf16[4,64,2048]{2,1,0:T(8,128)(2,1)} %copy-done.3, bf16[4,64,2048]{2,1,0:T(8,128)(2,1)} %copy-done.6, bf16[4,64,2048]{2,1,0:T(8,128)(2,1)} %copy-done.5, ...), custom_call_target="tpu_custom_call" | custom-call | flops 1342177280 | bytes 4718592 | tf_op jit(solution)/shard_map/mixed_back/pallas_call | solution.py:419
  254.6 27.6 %attend_back.1 = (bf16[640,3072]{1,0:T(8,128)(2,1)}, f32[2,2,1,1536]{3,2,1,0:T(1,128)}) custom-call(s32[1]{0:T(128)} %bitcast.me_ref, bf16[640,3072]{1,0:T(8,128)(2,1)} %get-tuple-element.40.qkv_ref, bf16[640,1024]{1,0:T(8,128)(2,1)} %mixed_back.1.grad_ref, s32[2,1,320]{2,1,0:T(1,128)} %broadcast_in_dim.4.seen_ref), custom_call_target="tpu_custom_call" | custom-call | flops 8388608000 | bytes 9830400 | tf_op jit(solution)/shard_map/attend_back/pallas_call | solution.py:469
  282.2 9.3 %qkv_grad_far.1 = bf16[2,2,4,64,1536]{4,3,2,1,0:T(8,128)(2,1)} custom-call(s32[1]{0:T(128)} %bitcast.me_ref, bf16[1024,640]{1,0:T(8,128)(2,1)} %get-tuple-element.55.turn_ref, bf16[640,3072]{1,0:T(8,128)(2,1)} %get-tuple-element.48.low_ref.right_ref), custom_call_target="tpu_custom_call" | custom-call | flops 2013265920 | bytes 11534336 | tf_op jit(solution)/shard_map/qkv_grad_far/pallas_call | solution.py:555
  291.5 10.4 %fc2_grad_far.1 = bf16[2,2,4,64,2048]{4,3,2,1,0:T(8,128)(2,1)} custom-call(s32[1]{0:T(128)} %bitcast.me_ref, bf16[1024,640]{1,0:T(8,128)(2,1)} %bitcast.168, bf16[640,4096]{1,0:T(8,128)(2,1)} %get-tuple-element.42.hid_ref.right_ref), custom_call_target="tpu_custom_call" | custom-call | flops 2684354560 | bytes 14942208 | tf_op jit(solution)/shard_map/fc2_grad_far/pallas_call | solution.py:555
  302.4 5.1 proj_grad_far.1
  309.2 10.4 %fc1_grad_far.1 = bf16[2,2,4,64,2048]{4,3,2,1,0:T(8,128)(2,1)} custom-call(s32[1]{0:T(128)} %bitcast.me_ref, bf16[1024,640]{1,0:T(8,128)(2,1)} %get-tuple-element.61.turn_ref, bf16[640,4096]{1,0:T(8,128)(2,1)} %get-tuple-element.46.low_ref.right_ref), custom_call_target="tpu_custom_call" | custom-call | flops 2684354560 | bytes 14942208 | tf_op jit(solution)/shard_map/fc1_grad_far/pallas_call | solution.py:555
  320.1 15.2 %norm_one_back.1 = (f32[640,1024]{1,0:T(8,128)}, f32[8,1024]{1,0:T(8,128)}) custom-call(s32[1]{0:T(128)} %bitcast.me_ref, bf16[640,3072]{1,0:T(8,128)(2,1)} %get-tuple-element.48.low_ref.right_ref, f32[640,1024]{1,0:T(8,128)} %bitcast.174, f32[640,1024]{1,0:T(8,128)} %get-tuple-element.49.base_ref, f32[8,1024]{1,0:T(8,128)} %reshape.152.table_ref, ...), custom_call_target="tpu_custom_call" | custom-call | flops 4026531840 | bytes 20709376 | tf_op jit(solution)/shard_map/norm_one_back/pallas_call | solution.py:380
  336.1 5.0 proj_grad_near.1
  341.2 3.0 collective-permute-start.48
  347.9 3.2 collective-permute-done.36
  352.5 3.5 collective-permute-done.37
  356.0 13.0 %collective-permute-start.38 = (f32[12,1024]{1,0:T(8,128)S(1)}, f32[12,1024]{1,0:T(8,128)S(1)}, u32[]{:S(2)}, u32[]{:S(2)}) collective-permute-start(f32[12,1024]{1,0:T(8,128)S(1)} %add.98), channel_id=1, source_target_pairs={{0,8},{1,9},{2,10},{3,11},{4,12},{5,13},{6,14},{7,15},{8,0},{9,1},... | collective-permute-start | bytes 147464 | tf_op jit(solution)/shard_map/ppermute | solution.py:570
  369.6 10.0 %qkv_grad_near.1 = (bf16[2,4,64,1536]{3,2,1,0:T(8,128)(2,1)}, bf16[2,4,64,1536]{3,2,1,0:T(8,128)(2,1)}) custom-call(s32[1]{0:T(128)} %bitcast.me_ref, bf16[1024,640]{1,0:T(8,128)(2,1)} %get-tuple-element.55.turn_ref, bf16[640,3072]{1,0:T(8,128)(2,1)} %get-tuple-element.48.low_ref.right_ref, bf16[2,2,4,64,1536]{4,3,2,1,0:T(8,128)(2,1)} %collective-permute-done.41.refs_0_), custom_call_target="tpu_custom_call" | custom-call | flops 2013265920 | bytes 11534336 | tf_op jit(solution)/shard_map/qkv_grad_near/pallas_call | solution.py:555
  380.6 2.0 collective-permute-start.40
  383.7 3.2 collective-permute-done.40
  386.9 5.0 collective-permute-done.49
  393.7 11.5 %fc2_grad_near.1 = (bf16[2,4,64,2048]{3,2,1,0:T(8,128)(2,1)}, bf16[2,4,64,2048]{3,2,1,0:T(8,128)(2,1)}) custom-call(s32[1]{0:T(128)} %bitcast.me_ref, bf16[1024,640]{1,0:T(8,128)(2,1)} %bitcast.169, bf16[640,4096]{1,0:T(8,128)(2,1)} %get-tuple-element.42.hid_ref.right_ref, bf16[2,2,4,64,2048]{4,3,2,1,0:T(8,128)(2,1)} %collective-permute-done.59.refs_0_), custom_call_target="tpu_custom_call" | custom-call | flops 2684354560 | bytes 14942208 | tf_op jit(solution)/shard_map/fc2_grad_near/pallas_call | solution.py:555
  407.5 2.3 add_convert_fusion.2
  420.1 11.4 %fc1_grad_near.1 = (bf16[2,4,64,2048]{3,2,1,0:T(8,128)(2,1)}, bf16[2,4,64,2048]{3,2,1,0:T(8,128)(2,1)}) custom-call(s32[1]{0:T(128)} %bitcast.me_ref, bf16[1024,640]{1,0:T(8,128)(2,1)} %get-tuple-element.61.turn_ref, bf16[640,4096]{1,0:T(8,128)(2,1)} %get-tuple-element.46.low_ref.right_ref, bf16[2,2,4,64,2048]{4,3,2,1,0:T(8,128)(2,1)} %collective-permute-done.53.refs_0_), custom_call_target="tpu_custom_call" | custom-call | flops 2684354560 | bytes 14942208 | tf_op jit(solution)/shard_map/fc1_grad_near/pallas_call | solution.py:555
  434.0 2.3 collective-permute-start.45
  442.7 30.8 %collective-permute-done.54 = bf16[2,4,64,2048]{3,2,1,0:T(8,128)(2,1)S(1)} collective-permute-done((bf16[2,4,64,2048]{3,2,1,0:T(8,128)(2,1)}, bf16[2,4,64,2048]{3,2,1,0:T(8,128)(2,1)S(1)}, u32[]{:S(2)}, u32[]{:S(2)}) %collective-permute-start.54) | collective-permute-done | bytes 2097184 | tf_op jit(solution)/shard_map/ppermute | solution.py:570
  484.2 6.4 %collective-permute-done.55 = bf16[4,64,2048]{2,1,0:T(8,128)(2,1)} collective-permute-done((bf16[4,64,2048]{2,1,0:T(8,128)(2,1)}, bf16[4,64,2048]{2,1,0:T(8,128)(2,1)}, u32[]{:S(2)}, u32[]{:S(2)}) %collective-permute-start.55) | collective-permute-done | bytes 1048608 | tf_op jit(solution)/shard_map/ppermute | solution.py:570
  494.8 1.9 collective-permute-start.58
  496.8 5.4 %collective-permute-done.63 = bf16[64,2048]{1,0:T(8,128)(2,1)S(1)} collective-permute-done((bf16[64,2048]{1,0:T(8,128)(2,1)S(1)}, bf16[64,2048]{1,0:T(8,128)(2,1)S(1)}, u32[]{:S(2)}, u32[]{:S(2)}) %collective-permute-start.63) | collective-permute-done | bytes 262176 | tf_op jit(solution)/shard_map/ppermute | solution.py:570
  504.4 18.9 %collective-permute-done.57 = bf16[64,2048]{1,0:T(8,128)(2,1)S(1)} collective-permute-done((bf16[64,2048]{1,0:T(8,128)(2,1)S(1)}, bf16[64,2048]{1,0:T(8,128)(2,1)S(1)}, u32[]{:S(2)}, u32[]{:S(2)}) %collective-permute-start.57) | collective-permute-done | bytes 262176 | tf_op jit(solution)/shard_map/ppermute | solution.py:570
  (237 shorter events, 89.9 us)
Async XLA Ops:
  2.8 34.7 %collective-permute-start.5 = (bf16[64,2048]{1,0:T(8,128)(2,1)S(1)}, bf16[64,2048]{1,0:T(8,128)(2,1)S(1)}, u32[]{:S(2)}, u32[]{:S(2)}) collective-permute-start(bf16[64,2048]{1,0:T(8,128)(2,1)S(1)} %pad_maximum_fusion.3), channel_id=1, source_target_pairs={{0,8},{1,9},{2,10},{3,11},{4,12},{5,13},{6,14},{7,15},{8,0},{9,1},... | collective-permute-start | bytes 786440 | tf_op jit(solution)/shard_map/ppermute | solution.py:570
  5.9 33.0 %collective-permute-start.6 = (bf16[64,2048]{1,0:T(8,128)(2,1)S(1)}, bf16[64,2048]{1,0:T(8,128)(2,1)S(1)}, u32[]{:S(2)}, u32[]{:S(2)}) collective-permute-start(bf16[64,2048]{1,0:T(8,128)(2,1)S(1)} %pad_maximum_fusion.3), channel_id=1, source_target_pairs={{0,16},{1,17},{2,18},{3,19},{4,20},{5,21},{6,22},{7,23},{8,24},{9,... | collective-permute-start | bytes 786440 | tf_op jit(solution)/shard_map/ppermute | solution.py:570
  8.5 30.4 %collective-permute-start.7 = (bf16[64,2048]{1,0:T(8,128)(2,1)S(1)}, bf16[64,2048]{1,0:T(8,128)(2,1)S(1)}, u32[]{:S(2)}, u32[]{:S(2)}) collective-permute-start(bf16[64,2048]{1,0:T(8,128)(2,1)S(1)} %pad_maximum_fusion.3), channel_id=1, source_target_pairs={{0,24},{1,25},{2,26},{3,27},{4,28},{5,29},{6,30},{7,31},{8,16},{9,... | collective-permute-start | bytes 786440 | tf_op jit(solution)/shard_map/ppermute | solution.py:570
  14.8 16.9 %collective-permute-start.1 = (f32[8,128]{1,0:T(8,128)S(1)}, f32[8,128]{1,0:T(8,128)S(1)}, u32[]{:S(2)}, u32[]{:S(2)}) collective-permute-start(f32[8,128]{1,0:T(8,128)S(1)} %get-tuple-element.114), channel_id=1, source_target_pairs={{0,16},{1,17},{2,18},{3,19},{4,20},{5,21},{6,22},{7,23},{8,24},{9,... | collective-permute-start | bytes 12296 | tf_op jit(solution)/shard_map/ppermute | solution.py:570
  35.5 21.3 %collective-permute-start.16 = (bf16[64,2048]{1,0:T(8,128)(2,1)S(1)}, bf16[64,2048]{1,0:T(8,128)(2,1)S(1)}, u32[]{:S(2)}, u32[]{:S(2)}) collective-permute-start(bf16[64,2048]{1,0:T(8,128)(2,1)S(1)} %convert_element_type.169), channel_id=1, source_target_pairs={{0,16},{1,17},{2,18},{3,19},{4,20},{5,21},{6,22},{7,23},{8,24},{9,... | collective-permute-start | bytes 786440 | tf_op jit(solution)/shard_map/ppermute | solution.py:570
  37.4 21.8 %collective-permute-start.17 = (bf16[64,2048]{1,0:T(8,128)(2,1)S(1)}, bf16[64,2048]{1,0:T(8,128)(2,1)S(1)}, u32[]{:S(2)}, u32[]{:S(2)}) collective-permute-start(bf16[64,2048]{1,0:T(8,128)(2,1)S(1)} %convert_element_type.169), channel_id=1, source_target_pairs={{0,24},{1,25},{2,26},{3,27},{4,28},{5,29},{6,30},{7,31},{8,16},{9,... | collective-permute-start | bytes 786440 | tf_op jit(solution)/shard_map/ppermute | solution.py:570
  39.0 42.5 %collective-permute-start.9 = (bf16[4,64,2048]{2,1,0:T(8,128)(2,1)S(1)}, bf16[4,64,2048]{2,1,0:T(8,128)(2,1)S(1)}, u32[]{:S(2)}, u32[]{:S(2)}) collective-permute-start(bf16[4,64,2048]{2,1,0:T(8,128)(2,1)S(1)} %pad_maximum_fusion.refs_0_), channel_id=1, source_target_pairs={{0,1},{1,0},{2,6},{3,7},{4,5},{5,4},{6,2},{7,3},{8,9},{9,8},{10,14... | collective-permute-start | bytes 3145736 | tf_op jit(solution)/shard_map/ppermute | solution.py:570
  40.6 20.3 %collective-permute-start.25 = (bf16[64,2048]{1,0:T(8,128)(2,1)S(1)}, bf16[64,2048]{1,0:T(8,128)(2,1)S(1)}, u32[]{:S(2)}, u32[]{:S(2)}) collective-permute-start(bf16[64,2048]{1,0:T(8,128)(2,1)S(1)} %get-tuple-element.90), channel_id=1, source_target_pairs={{0,8},{1,9},{2,10},{3,11},{4,12},{5,13},{6,14},{7,15},{8,0},{9,1},... | collective-permute-start | bytes 786440 | tf_op jit(solution)/shard_map/ppermute | solution.py:570
  46.5 32.3 %collective-permute-start.26 = (bf16[64,2048]{1,0:T(8,128)(2,1)S(1)}, bf16[64,2048]{1,0:T(8,128)(2,1)S(1)}, u32[]{:S(2)}, u32[]{:S(2)}) collective-permute-start(bf16[64,2048]{1,0:T(8,128)(2,1)S(1)} %get-tuple-element.90), channel_id=1, source_target_pairs={{0,16},{1,17},{2,18},{3,19},{4,20},{5,21},{6,22},{7,23},{8,24},{9,... | collective-permute-start | bytes 786440 | tf_op jit(solution)/shard_map/ppermute | solution.py:570
  56.8 23.6 %collective-permute-start.27 = (bf16[64,2048]{1,0:T(8,128)(2,1)S(1)}, bf16[64,2048]{1,0:T(8,128)(2,1)S(1)}, u32[]{:S(2)}, u32[]{:S(2)}) collective-permute-start(bf16[64,2048]{1,0:T(8,128)(2,1)S(1)} %get-tuple-element.90), channel_id=1, source_target_pairs={{0,24},{1,25},{2,26},{3,27},{4,28},{5,29},{6,30},{7,31},{8,16},{9,... | collective-permute-start | bytes 786440 | tf_op jit(solution)/shard_map/ppermute | solution.py:570
  59.2 23.5 %collective-permute-start.8 = (bf16[4,64,2048]{2,1,0:T(8,128)(2,1)S(1)}, bf16[4,64,2048]{2,1,0:T(8,128)(2,1)S(1)}, u32[]{:S(2)}, u32[]{:S(2)}) collective-permute-start(bf16[4,64,2048]{2,1,0:T(8,128)(2,1)S(1)} %pad_maximum_fusion.refs_0_), channel_id=1, source_target_pairs={{0,4},{1,5},{2,3},{3,2},{4,0},{5,1},{6,7},{7,6},{8,12},{9,13},{10,... | collective-permute-start | bytes 3145736 | tf_op jit(solution)/shard_map/ppermute | solution.py:570
  60.9 22.4 %collective-permute-start.11 = (bf16[4,64,2048]{2,1,0:T(8,128)(2,1)S(1)}, bf16[4,64,2048]{2,1,0:T(8,128)(2,1)S(1)}, u32[]{:S(2)}, u32[]{:S(2)}) collective-permute-start(bf16[4,64,2048]{2,1,0:T(8,128)(2,1)S(1)} %pad_maximum_fusion.refs_0_), channel_id=1, source_target_pairs={{0,2},{1,3},{2,0},{3,1},{4,6},{5,7},{6,4},{7,5},{8,10},{9,11},{10,... | collective-permute-start | bytes 3145736 | tf_op jit(solution)/shard_map/ppermute | solution.py:570
  78.8 26.1 %collective-permute-start.19 = (bf16[4,64,2048]{2,1,0:T(8,128)(2,1)S(1)}, bf16[4,64,2048]{2,1,0:T(8,128)(2,1)}, u32[]{:S(2)}, u32[]{:S(2)}) collective-permute-start(bf16[4,64,2048]{2,1,0:T(8,128)(2,1)S(1)} %pad_maximum_fusion.1.refs_0_), channel_id=1, source_target_pairs={{0,1},{1,0},{2,6},{3,7},{4,5},{5,4},{6,2},{7,3},{8,9},{9,8},{10,14... | collective-permute-start | bytes 3145736 | tf_op jit(solution)/shard_map/ppermute | solution.py:570
  80.4 26.1 %collective-permute-start.18 = (bf16[4,64,2048]{2,1,0:T(8,128)(2,1)S(1)}, bf16[4,64,2048]{2,1,0:T(8,128)(2,1)}, u32[]{:S(2)}, u32[]{:S(2)}) collective-permute-start(bf16[4,64,2048]{2,1,0:T(8,128)(2,1)S(1)} %pad_maximum_fusion.1.refs_0_), channel_id=1, source_target_pairs={{0,4},{1,5},{2,3},{3,2},{4,0},{5,1},{6,7},{7,6},{8,12},{9,13},{10,... | collective-permute-start | bytes 3145736 | tf_op jit(solution)/shard_map/ppermute | solution.py:570
  81.4 25.1 %collective-permute-start.21 = (bf16[4,64,2048]{2,1,0:T(8,128)(2,1)S(1)}, bf16[4,64,2048]{2,1,0:T(8,128)(2,1)S(1)}, u32[]{:S(2)}, u32[]{:S(2)}) collective-permute-start(bf16[4,64,2048]{2,1,0:T(8,128)(2,1)S(1)} %pad_maximum_fusion.1.refs_0_), channel_id=1, source_target_pairs={{0,2},{1,3},{2,0},{3,1},{4,6},{5,7},{6,4},{7,5},{8,10},{9,11},{10,... | collective-permute-start | bytes 3145736 | tf_op jit(solution)/shard_map/ppermute | solution.py:570
  82.7 44.6 %collective-permute-start.29 = (bf16[4,64,2048]{2,1,0:T(8,128)(2,1)}, bf16[4,64,2048]{2,1,0:T(8,128)(2,1)S(1)}, u32[]{:S(2)}, u32[]{:S(2)}) collective-permute-start(bf16[4,64,2048]{2,1,0:T(8,128)(2,1)} %pad_maximum_fusion.2.refs_0_), channel_id=1, source_target_pairs={{0,1},{1,0},{2,6},{3,7},{4,5},{5,4},{6,2},{7,3},{8,9},{9,8},{10,14... | collective-permute-start | bytes 3145736 | tf_op jit(solution)/shard_map/ppermute | solution.py:570
  83.3 46.2 %collective-permute-start.28 = (bf16[4,64,2048]{2,1,0:T(8,128)(2,1)}, bf16[4,64,2048]{2,1,0:T(8,128)(2,1)}, u32[]{:S(2)}, u32[]{:S(2)}) collective-permute-start(bf16[4,64,2048]{2,1,0:T(8,128)(2,1)} %pad_maximum_fusion.2.refs_0_), channel_id=1, source_target_pairs={{0,4},{1,5},{2,3},{3,2},{4,0},{5,1},{6,7},{7,6},{8,12},{9,13},{10,... | collective-permute-start | bytes 3145736 | tf_op jit(solution)/shard_map/ppermute | solution.py:570
  105.0 26.7 %collective-permute-start.10 = (bf16[4,64,2048]{2,1,0:T(8,128)(2,1)S(1)}, bf16[4,64,2048]{2,1,0:T(8,128)(2,1)}, u32[]{:S(2)}, u32[]{:S(2)}) collective-permute-start(bf16[4,64,2048]{2,1,0:T(8,128)(2,1)S(1)} %collective-permute-done.9.refs_2_), channel_id=1, source_target_pairs={{0,4},{1,5},{2,3},{3,2},{4,0},{5,1},{6,7},{7,6},{8,12},{9,13},{10,... | collective-permute-start | bytes 3145736 | tf_op jit(solution)/shard_map/ppermute | solution.py:570
  106.5 26.1 %collective-permute-start.13 = (bf16[4,64,2048]{2,1,0:T(8,128)(2,1)S(1)}, bf16[4,64,2048]{2,1,0:T(8,128)(2,1)S(1)}, u32[]{:S(2)}, u32[]{:S(2)}) collective-permute-start(bf16[4,64,2048]{2,1,0:T(8,128)(2,1)S(1)} %collective-permute-done.9.refs_2_), channel_id=1, source_target_pairs={{0,2},{1,3},{2,0},{3,1},{4,6},{5,7},{6,4},{7,5},{8,10},{9,11},{10,... | collective-permute-start | bytes 3145736 | tf_op jit(solution)/shard_map/ppermute | solution.py:570
  106.5 27.0 %collective-permute-start.12 = (bf16[4,64,2048]{2,1,0:T(8,128)(2,1)S(1)}, bf16[4,64,2048]{2,1,0:T(8,128)(2,1)}, u32[]{:S(2)}, u32[]{:S(2)}) collective-permute-start(bf16[4,64,2048]{2,1,0:T(8,128)(2,1)S(1)} %collective-permute-done.8.refs_1_), channel_id=1, source_target_pairs={{0,2},{1,3},{2,0},{3,1},{4,6},{5,7},{6,4},{7,5},{8,10},{9,11},{10,... | collective-permute-start | bytes 3145736 | tf_op jit(solution)/shard_map/ppermute | solution.py:570
  128.4 15.1 %collective-permute-start.20 = (bf16[4,64,2048]{2,1,0:T(8,128)(2,1)}, bf16[4,64,2048]{2,1,0:T(8,128)(2,1)}, u32[]{:S(2)}, u32[]{:S(2)}) collective-permute-start(bf16[4,64,2048]{2,1,0:T(8,128)(2,1)} %collective-permute-done.19.refs_2_), channel_id=1, source_target_pairs={{0,4},{1,5},{2,3},{3,2},{4,0},{5,1},{6,7},{7,6},{8,12},{9,13},{10,... | collective-permute-start | bytes 3145736 | tf_op jit(solution)/shard_map/ppermute | solution.py:570
  129.4 16.4 %collective-permute-start.23 = (bf16[4,64,2048]{2,1,0:T(8,128)(2,1)}, bf16[4,64,2048]{2,1,0:T(8,128)(2,1)}, u32[]{:S(2)}, u32[]{:S(2)}) collective-permute-start(bf16[4,64,2048]{2,1,0:T(8,128)(2,1)} %collective-permute-done.19.refs_2_), channel_id=1, source_target_pairs={{0,2},{1,3},{2,0},{3,1},{4,6},{5,7},{6,4},{7,5},{8,10},{9,11},{10,... | collective-permute-start | bytes 3145736 | tf_op jit(solution)/shard_map/ppermute | solution.py:570
  132.6 22.1 %collective-permute-start.30 = (bf16[4,64,2048]{2,1,0:T(8,128)(2,1)}, bf16[4,64,2048]{2,1,0:T(8,128)(2,1)}, u32[]{:S(2)}, u32[]{:S(2)}) collective-permute-start(bf16[4,64,2048]{2,1,0:T(8,128)(2,1)} %copy-done.23), channel_id=1, source_target_pairs={{0,4},{1,5},{2,3},{3,2},{4,0},{5,1},{6,7},{7,6},{8,12},{9,13},{10,... | collective-permute-start | bytes 3145736 | tf_op jit(solution)/shard_map/ppermute | solution.py:570
  133.5 21.3 %collective-permute-start.14 = (bf16[4,64,2048]{2,1,0:T(8,128)(2,1)}, bf16[4,64,2048]{2,1,0:T(8,128)(2,1)}, u32[]{:S(2)}, u32[]{:S(2)}) collective-permute-start(bf16[4,64,2048]{2,1,0:T(8,128)(2,1)} %collective-permute-done.10.refs_3_), channel_id=1, source_target_pairs={{0,2},{1,3},{2,0},{3,1},{4,6},{5,7},{6,4},{7,5},{8,10},{9,11},{10,... | collective-permute-start | bytes 3145736 | tf_op jit(solution)/shard_map/ppermute | solution.py:570
  143.5 50.1 %collective-permute-start.24 = (bf16[4,64,2048]{2,1,0:T(8,128)(2,1)}, bf16[4,64,2048]{2,1,0:T(8,128)(2,1)S(1)}, u32[]{:S(2)}, u32[]{:S(2)}) collective-permute-start(bf16[4,64,2048]{2,1,0:T(8,128)(2,1)} %collective-permute-done.20.refs_3_), channel_id=1, source_target_pairs={{0,2},{1,3},{2,0},{3,1},{4,6},{5,7},{6,4},{7,5},{8,10},{9,11},{10,... | collective-permute-start | bytes 3145736 | tf_op jit(solution)/shard_map/ppermute | solution.py:570
  145.9 64.9 %collective-permute-start.31 = (bf16[4,64,2048]{2,1,0:T(8,128)(2,1)}, bf16[4,64,2048]{2,1,0:T(8,128)(2,1)}, u32[]{:S(2)}, u32[]{:S(2)}) collective-permute-start(bf16[4,64,2048]{2,1,0:T(8,128)(2,1)} %pad_maximum_fusion.2.refs_0_), channel_id=1, source_target_pairs={{0,2},{1,3},{2,0},{3,1},{4,6},{5,7},{6,4},{7,5},{8,10},{9,11},{10,... | collective-permute-start | bytes 3145736 | tf_op jit(solution)/shard_map/ppermute | solution.py:570
  146.0 64.8 %collective-permute-start.33 = (bf16[4,64,2048]{2,1,0:T(8,128)(2,1)}, bf16[4,64,2048]{2,1,0:T(8,128)(2,1)}, u32[]{:S(2)}, u32[]{:S(2)}) collective-permute-start(bf16[4,64,2048]{2,1,0:T(8,128)(2,1)} %copy-done.23), channel_id=1, source_target_pairs={{0,2},{1,3},{2,0},{3,1},{4,6},{5,7},{6,4},{7,5},{8,10},{9,11},{10,... | collective-permute-start | bytes 3145736 | tf_op jit(solution)/shard_map/ppermute | solution.py:570
  154.7 56.1 %collective-permute-start.32 = (bf16[4,64,2048]{2,1,0:T(8,128)(2,1)}, bf16[4,64,2048]{2,1,0:T(8,128)(2,1)}, u32[]{:S(2)}, u32[]{:S(2)}) collective-permute-start(bf16[4,64,2048]{2,1,0:T(8,128)(2,1)} %collective-permute-done.28.refs_1_), channel_id=1, source_target_pairs={{0,2},{1,3},{2,0},{3,1},{4,6},{5,7},{6,4},{7,5},{8,10},{9,11},{10,... | collective-permute-start | bytes 3145736 | tf_op jit(solution)/shard_map/ppermute | solution.py:570
  154.8 56.0 %collective-permute-start.34 = (bf16[4,64,2048]{2,1,0:T(8,128)(2,1)}, bf16[4,64,2048]{2,1,0:T(8,128)(2,1)}, u32[]{:S(2)}, u32[]{:S(2)}) collective-permute-start(bf16[4,64,2048]{2,1,0:T(8,128)(2,1)} %collective-permute-done.30.refs_3_), channel_id=1, source_target_pairs={{0,2},{1,3},{2,0},{3,1},{4,6},{5,7},{6,4},{7,5},{8,10},{9,11},{10,... | collective-permute-start | bytes 3145736 | tf_op jit(solution)/shard_map/ppermute | solution.py:570
  291.5 77.5 %collective-permute-start.41 = (bf16[2,2,4,64,1536]{4,3,2,1,0:T(8,128)(2,1)}, bf16[2,2,4,64,1536]{4,3,2,1,0:T(8,128)(2,1)}, u32[]{:S(2)}, u32[]{:S(2)}) collective-permute-start(bf16[2,2,4,64,1536]{4,3,2,1,0:T(8,128)(2,1)} %qkv_grad_far.1), channel_id=1, source_target_pairs={{0,2},{1,3},{2,0},{3,1},{4,6},{5,7},{6,4},{7,5},{8,10},{9,11},{10,... | collective-permute-start | bytes 9437192 | tf_op jit(solution)/shard_map/ppermute | solution.py:570
  302.0 91.7 %collective-permute-start.59 = (bf16[2,2,4,64,2048]{4,3,2,1,0:T(8,128)(2,1)}, bf16[2,2,4,64,2048]{4,3,2,1,0:T(8,128)(2,1)}, u32[]{:S(2)}, u32[]{:S(2)}) collective-permute-start(bf16[2,2,4,64,2048]{4,3,2,1,0:T(8,128)(2,1)} %fc2_grad_far.1), channel_id=1, source_target_pairs={{0,2},{1,3},{2,0},{3,1},{4,6},{5,7},{6,4},{7,5},{8,10},{9,11},{10,... | collective-permute-start | bytes 12582920 | tf_op jit(solution)/shard_map/ppermute | solution.py:570
  307.5 28.6 %collective-permute-start.47 = (bf16[2,2,4,64,512]{4,3,2,1,0:T(8,128)(2,1)}, bf16[2,2,4,64,512]{4,3,2,1,0:T(8,128)(2,1)}, u32[]{:S(2)}, u32[]{:S(2)}) collective-permute-start(bf16[2,2,4,64,512]{4,3,2,1,0:T(8,128)(2,1)} %proj_grad_far.1), channel_id=1, source_target_pairs={{0,2},{1,3},{2,0},{3,1},{4,6},{5,7},{6,4},{7,5},{8,10},{9,11},{10,... | collective-permute-start | bytes 3145736 | tf_op jit(solution)/shard_map/ppermute | solution.py:570
  319.6 100.4 %collective-permute-start.53 = (bf16[2,2,4,64,2048]{4,3,2,1,0:T(8,128)(2,1)}, bf16[2,2,4,64,2048]{4,3,2,1,0:T(8,128)(2,1)}, u32[]{:S(2)}, u32[]{:S(2)}) collective-permute-start(bf16[2,2,4,64,2048]{4,3,2,1,0:T(8,128)(2,1)} %fc1_grad_far.1), channel_id=1, source_target_pairs={{0,2},{1,3},{2,0},{3,1},{4,6},{5,7},{6,4},{7,5},{8,10},{9,11},{10,... | collective-permute-start | bytes 12582920 | tf_op jit(solution)/shard_map/ppermute | solution.py:570
  341.2 38.4 %collective-permute-start.48 = (bf16[2,4,64,512]{3,2,1,0:T(8,128)(2,1)}, bf16[2,4,64,512]{3,2,1,0:T(8,128)(2,1)S(1)}, u32[]{:S(2)}, u32[]{:S(2)}) collective-permute-start(bf16[2,4,64,512]{3,2,1,0:T(8,128)(2,1)} %get-tuple-element.60), channel_id=1, source_target_pairs={{0,1},{1,0},{2,6},{3,7},{4,5},{5,4},{6,2},{7,3},{8,9},{9,8},{10,14... | collective-permute-start | bytes 1572872 | tf_op jit(solution)/shard_map/ppermute | solution.py:570
  356.0 24.6 %collective-permute-start.38 = (f32[12,1024]{1,0:T(8,128)S(1)}, f32[12,1024]{1,0:T(8,128)S(1)}, u32[]{:S(2)}, u32[]{:S(2)}) collective-permute-start(f32[12,1024]{1,0:T(8,128)S(1)} %add.98), channel_id=1, source_target_pairs={{0,8},{1,9},{2,10},{3,11},{4,12},{5,13},{6,14},{7,15},{8,0},{9,1},... | collective-permute-start | bytes 147464 | tf_op jit(solution)/shard_map/ppermute | solution.py:570
  379.6 26.7 %collective-permute-start.42 = (bf16[2,4,64,1536]{3,2,1,0:T(8,128)(2,1)}, bf16[2,4,64,1536]{3,2,1,0:T(8,128)(2,1)S(1)}, u32[]{:S(2)}, u32[]{:S(2)}) collective-permute-start(bf16[2,4,64,1536]{3,2,1,0:T(8,128)(2,1)} %get-tuple-element.57), channel_id=1, source_target_pairs={{0,1},{1,0},{2,6},{3,7},{4,5},{5,4},{6,2},{7,3},{8,9},{9,8},{10,14... | collective-permute-start | bytes 4718600 | tf_op jit(solution)/shard_map/ppermute | solution.py:570
  392.6 20.7 %collective-permute-start.50 = (bf16[64,512]{1,0:T(8,128)(2,1)}, bf16[64,512]{1,0:T(8,128)(2,1)S(1)}, u32[]{:S(2)}, u32[]{:S(2)}) collective-permute-start(bf16[64,512]{1,0:T(8,128)(2,1)} %get-tuple-element.94), channel_id=1, source_target_pairs={{0,8},{1,9},{2,10},{3,11},{4,12},{5,13},{6,14},{7,15},{8,0},{9,1},... | collective-permute-start | bytes 196616 | tf_op jit(solution)/shard_map/ppermute | solution.py:570
  405.1 34.7 %collective-permute-start.60 = (bf16[2,4,64,2048]{3,2,1,0:T(8,128)(2,1)}, bf16[2,4,64,2048]{3,2,1,0:T(8,128)(2,1)S(1)}, u32[]{:S(2)}, u32[]{:S(2)}) collective-permute-start(bf16[2,4,64,2048]{3,2,1,0:T(8,128)(2,1)} %get-tuple-element.65), channel_id=1, source_target_pairs={{0,1},{1,0},{2,6},{3,7},{4,5},{5,4},{6,2},{7,3},{8,9},{9,8},{10,14... | collective-permute-start | bytes 6291464 | tf_op jit(solution)/shard_map/ppermute | solution.py:570
  410.8 21.5 %collective-permute-start.43 = (bf16[4,64,1536]{2,1,0:T(8,128)(2,1)}, bf16[4,64,1536]{2,1,0:T(8,128)(2,1)}, u32[]{:S(2)}, u32[]{:S(2)}) collective-permute-start(bf16[4,64,1536]{2,1,0:T(8,128)(2,1)} %slice_bitcast_fusion.4), channel_id=1, source_target_pairs={{0,4},{1,5},{2,3},{3,2},{4,0},{5,1},{6,7},{7,6},{8,12},{9,13},{10,... | collective-permute-start | bytes 2359304 | tf_op jit(solution)/shard_map/ppermute | solution.py:570
  431.5 42.0 %collective-permute-start.54 = (bf16[2,4,64,2048]{3,2,1,0:T(8,128)(2,1)}, bf16[2,4,64,2048]{3,2,1,0:T(8,128)(2,1)S(1)}, u32[]{:S(2)}, u32[]{:S(2)}) collective-permute-start(bf16[2,4,64,2048]{3,2,1,0:T(8,128)(2,1)} %get-tuple-element.63), channel_id=1, source_target_pairs={{0,1},{1,0},{2,6},{3,7},{4,5},{5,4},{6,2},{7,3},{8,9},{9,8},{10,14... | collective-permute-start | bytes 6291464 | tf_op jit(solution)/shard_map/ppermute | solution.py:570
  433.7 42.8 %collective-permute-start.44 = (bf16[64,1536]{1,0:T(8,128)(2,1)S(1)}, bf16[64,1536]{1,0:T(8,128)(2,1)S(1)}, u32[]{:S(2)}, u32[]{:S(2)}) collective-permute-start(bf16[64,1536]{1,0:T(8,128)(2,1)S(1)} %get-tuple-element.86), channel_id=1, source_target_pairs={{0,8},{1,9},{2,10},{3,11},{4,12},{5,13},{6,14},{7,15},{8,0},{9,1},... | collective-permute-start | bytes 589832 | tf_op jit(solution)/shard_map/ppermute | solution.py:570
  434.0 42.5 %collective-permute-start.45 = (bf16[64,1536]{1,0:T(8,128)(2,1)S(1)}, bf16[64,1536]{1,0:T(8,128)(2,1)S(1)}, u32[]{:S(2)}, u32[]{:S(2)}) collective-permute-start(bf16[64,1536]{1,0:T(8,128)(2,1)S(1)} %get-tuple-element.88), channel_id=1, source_target_pairs={{0,16},{1,17},{2,18},{3,19},{4,20},{5,21},{6,22},{7,23},{8,24},{9,... | collective-permute-start | bytes 589832 | tf_op jit(solution)/shard_map/ppermute | solution.py:570
  436.3 40.2 %collective-permute-start.46 = (bf16[64,1536]{1,0:T(8,128)(2,1)S(1)}, bf16[64,1536]{1,0:T(8,128)(2,1)S(1)}, u32[]{:S(2)}, u32[]{:S(2)}) collective-permute-start(bf16[64,1536]{1,0:T(8,128)(2,1)S(1)} %get-tuple-element.87), channel_id=1, source_target_pairs={{0,24},{1,25},{2,26},{3,27},{4,28},{5,29},{6,30},{7,31},{8,16},{9,... | collective-permute-start | bytes 589832 | tf_op jit(solution)/shard_map/ppermute | solution.py:570
  441.7 36.1 %collective-permute-start.61 = (bf16[4,64,2048]{2,1,0:T(8,128)(2,1)}, bf16[4,64,2048]{2,1,0:T(8,128)(2,1)}, u32[]{:S(2)}, u32[]{:S(2)}) collective-permute-start(bf16[4,64,2048]{2,1,0:T(8,128)(2,1)} %slice_bitcast_fusion), channel_id=1, source_target_pairs={{0,4},{1,5},{2,3},{3,2},{4,0},{5,1},{6,7},{7,6},{8,12},{9,13},{10,... | collective-permute-start | bytes 3145736 | tf_op jit(solution)/shard_map/ppermute | solution.py:570
  480.8 21.3 %collective-permute-start.63 = (bf16[64,2048]{1,0:T(8,128)(2,1)S(1)}, bf16[64,2048]{1,0:T(8,128)(2,1)S(1)}, u32[]{:S(2)}, u32[]{:S(2)}) collective-permute-start(bf16[64,2048]{1,0:T(8,128)(2,1)S(1)} %get-tuple-element.82), channel_id=1, source_target_pairs={{0,16},{1,17},{2,18},{3,19},{4,20},{5,21},{6,22},{7,23},{8,24},{9,... | collective-permute-start | bytes 786440 | tf_op jit(solution)/shard_map/ppermute | solution.py:570
  482.3 19.8 %collective-permute-start.64 = (bf16[64,2048]{1,0:T(8,128)(2,1)S(1)}, bf16[64,2048]{1,0:T(8,128)(2,1)S(1)}, u32[]{:S(2)}, u32[]{:S(2)}) collective-permute-start(bf16[64,2048]{1,0:T(8,128)(2,1)S(1)} %get-tuple-element.81), channel_id=1, source_target_pairs={{0,24},{1,25},{2,26},{3,27},{4,28},{5,29},{6,30},{7,31},{8,16},{9,... | collective-permute-start | bytes 786440 | tf_op jit(solution)/shard_map/ppermute | solution.py:570
  493.4 29.9 %collective-permute-start.57 = (bf16[64,2048]{1,0:T(8,128)(2,1)S(1)}, bf16[64,2048]{1,0:T(8,128)(2,1)S(1)}, u32[]{:S(2)}, u32[]{:S(2)}) collective-permute-start(bf16[64,2048]{1,0:T(8,128)(2,1)S(1)} %get-tuple-element.85), channel_id=1, source_target_pairs={{0,16},{1,17},{2,18},{3,19},{4,20},{5,21},{6,22},{7,23},{8,24},{9,... | collective-permute-start | bytes 786440 | tf_op jit(solution)/shard_map/ppermute | solution.py:570
  494.8 28.4 %collective-permute-start.58 = (bf16[64,2048]{1,0:T(8,128)(2,1)S(1)}, bf16[64,2048]{1,0:T(8,128)(2,1)S(1)}, u32[]{:S(2)}, u32[]{:S(2)}) collective-permute-start(bf16[64,2048]{1,0:T(8,128)(2,1)S(1)} %get-tuple-element.84), channel_id=1, source_target_pairs={{0,24},{1,25},{2,26},{3,27},{4,28},{5,29},{6,30},{7,31},{8,16},{9,... | collective-permute-start | bytes 786440 | tf_op jit(solution)/shard_map/ppermute | solution.py:570
  (43 other events, 825.8 us)

commit v2 on v1

--- a/solution.py
+++ b/solution.py
@@ -44,7 +44,7 @@
         ),
         out_shape=shapes,
         compiler_params=pltpu.CompilerParams(
-            dimension_semantics=("arbitrary",) * len(grid), vmem_limit_bytes=60 << 20
+            dimension_semantics=("arbitrary",) * len(grid), vmem_limit_bytes=32 << 20
         ),
         cost_estimate=pl.CostEstimate(flops=flops, bytes_accessed=moved, transcendentals=0),
         name=name,
@@ -145,12 +145,6 @@
     return lane < HEAD_DIM, lane >= HEAD_DIM
 
 
-def soft(query, key, seen):
-    scores = jnp.where(seen, mm_nt(query, key) * HEAD_DIM**-0.5, masked_score)
-    exps = jnp.exp(scores - jnp.max(scores, axis=-1, keepdims=True))
-    return exps / jnp.sum(exps, axis=-1, keepdims=True)
-
-
 def attend_call(me, qkv, visible):
     images, _, seq = visible.shape
     count, full = qkv.shape
@@ -159,18 +153,18 @@
     def body(me_ref, qkv_ref, seen_ref, out_ref):
         seen = seen_ref[0] > 0
 
-        @pl.loop(0, half // TILE)
-        def _(pair):
-            col = pl.multiple_of(pair * TILE, TILE)
-            query = qkv_ref[:, pl.ds(col, TILE)]
-            key = qkv_ref[:, pl.ds(half + col, TILE)]
-            value = qkv_ref[:, pl.ds(2 * half + col, TILE)]
+        for col in range(0, half, TILE):
+            query = qkv_ref[:, col : col + TILE] * jnp.asarray(HEAD_DIM**-0.5, LOW)
+            key = qkv_ref[:, half + col : half + col + TILE]
+            value = qkv_ref[:, 2 * half + col : 2 * half + col + TILE]
             lanes = head_halves(query.shape)
             mixed = []
             for keep in lanes:
-                probs = soft(jnp.where(keep, query, 0), key, seen)
-                mixed.append(mm(probs.astype(LOW), value))
-            out_ref[:, pl.ds(col, TILE)] = jnp.where(lanes[0], mixed[0], mixed[1]).astype(LOW)
+                scores = jnp.where(seen, mm_nt(jnp.where(keep, query, 0), key), masked_score)
+                exps = jnp.exp(scores - jnp.max(scores, axis=-1, keepdims=True))
+                total = jnp.sum(exps, axis=-1, keepdims=True)
+                mixed.append(mm(exps.astype(LOW), value) * (1.0 / total))
+            out_ref[:, col : col + TILE] = jnp.where(lanes[0], mixed[0], mixed[1]).astype(LOW)
 
     return call(
         body,
@@ -430,41 +424,39 @@
 
 
 def attend_back_call(me, qkv, grads, visible):
-    images, _, seq = visible.shape
+    images, seq, _ = visible.shape
     count, full = qkv.shape
     half = full // 6
     scale = HEAD_DIM**-0.5
 
     def body(me_ref, qkv_ref, grad_ref, seen_ref, out_ref, sum_ref):
         seen = seen_ref[0] > 0
-
-        @pl.loop(0, half // TILE)
-        def _(pair):
-            col = pl.multiple_of(pair * TILE, TILE)
-            query = qkv_ref[:, pl.ds(col, TILE)]
-            key = qkv_ref[:, pl.ds(half + col, TILE)]
-            value = qkv_ref[:, pl.ds(2 * half + col, TILE)]
-            grad = grad_ref[:, pl.ds(col, TILE)]
+        for col in range(0, half, TILE):
+            query = qkv_ref[:, col : col + TILE] * jnp.asarray(scale, LOW)
+            key = qkv_ref[:, half + col : half + col + TILE]
+            value = qkv_ref[:, 2 * half + col : 2 * half + col + TILE]
+            grad = grad_ref[:, col : col + TILE]
             lanes = head_halves(query.shape)
             parts = []
             for keep in lanes:
-                probs = soft(jnp.where(keep, query, 0), key, seen)
-                prob_grad = mm_nt(jnp.where(keep, grad, 0), value)
-                row_dot = jnp.sum(probs * prob_grad, axis=-1, keepdims=True)
+                scores = jnp.where(seen, mm_nt(jnp.where(keep, key, 0), query), masked_score)
+                exps = jnp.exp(scores - jnp.max(scores, axis=0, keepdims=True))
+                probs = exps * (1.0 / jnp.sum(exps, axis=0, keepdims=True))
+                prob_grad = mm_nt(jnp.where(keep, value, 0), grad)
+                row_dot = jnp.sum(probs * prob_grad, axis=0, keepdims=True)
                 score_grad = (probs * (prob_grad - row_dot)).astype(LOW)
                 parts.append(
                     (
-                        mm(score_grad, key) * scale,
-                        mm_tn(score_grad, query) * scale,
-                        mm_tn(probs.astype(LOW), grad),
+                        mm_tn(key, score_grad).T * scale,
+                        mm(score_grad, query),
+                        mm(probs.astype(LOW), grad),
                     )
                 )
             for at in range(3):
                 merged = jnp.where(lanes[0], parts[0][at], parts[1][at])
-                out_ref[:, pl.ds(at * half + col, TILE)] = merged.astype(LOW)
-                sum_ref[0, 0, :, pl.ds(at * half + col, TILE)] = jnp.sum(
-                    merged, axis=0, keepdims=True
-                )
+                put = at * half + col
+                out_ref[:, put : put + TILE] = merged.astype(LOW)
+                sum_ref[0, 0, :, put : put + TILE] = jnp.sum(merged, axis=0, keepdims=True)
 
     return call(
         body,
@@ -472,7 +464,7 @@
         [
             pl.BlockSpec((seq, 3 * half), lambda i, y, me: (i, y)),
             pl.BlockSpec((seq, half), lambda i, y, me: (i, y)),
-            pl.BlockSpec((1, 1, seq), lambda i, y, me: (i, 0, 0)),
+            pl.BlockSpec((1, seq, 1), lambda i, y, me: (i, 0, 0)),
         ],
         [
             pl.BlockSpec((seq, 3 * half), lambda i, y, me: (i, y)),
@@ -494,71 +486,111 @@
     span = right.shape[1] // 2
     chunk = next(c for c in (1024, 768, 512, 384, 256, 128) if span % c == 0)
     parts = span // chunk
+    steps = 2 * parts
     rows = width // (4 * depth)
-
-    def spot(t):
-        first = 1 - t // (2 * parts)
-        return first, t // parts % 2, t % parts
+    quarter = width // 4
+
+    def body(me_ref, turn_ref, right_ref, *refs):
+        if core_flip:
+            (far_ref, lefts, ready, sems) = refs
+        else:
+            (got_ref, kept_ref, sent_ref, lefts, ready, sems, got, got_sems) = refs
+        step = pl.program_id(0)
+        slot = step % 2
+        owner = ((me_ref[0] >> 1) & 1) ^ core_flip
+
+        def spot(off_y, off_x):
+            return jnp.where(owner == 0, off_y, off_x), jnp.where(owner == 0, off_x, off_y)
+
+        def fetched(at, off_x):
+            first, second = spot(1 - at // parts, off_x)
+            col = pl.multiple_of(at % parts * chunk, chunk)
+            return pltpu.make_async_copy(
+                got_ref.at[first, second, :, :, pl.ds(col, chunk)],
+                got.at[at, off_x],
+                got_sems.at[at, off_x],
+            )
+
+        def leaving(target, at, off_x):
+            col = pl.multiple_of(at % parts * chunk, chunk)
+            return pltpu.make_async_copy(
+                ready.at[at % 2, off_x],
+                target.at[:, :, pl.ds(col, chunk)],
+                sems.at[at % 2, off_x],
+            )
+
+        @pl.when(step == 0)
+        def _():
+            if not core_flip:
+                for at in range(steps):
+                    for off_x in range(2):
+                        fetched(at, off_x).start()
+            for off_x in range(2):
+                for off_z in range(depth):
+                    row = pl.multiple_of(dp_of(me_ref[0], core_flip, off_x, off_z) * rows, rows)
+                    put = off_x * quarter + off_z * rows
+                    lefts[put : put + rows, :] = turn_ref[pl.ds(row, rows), :]
+
+        product = mm(lefts[...], right_ref[...]).reshape(2, depth, rows, chunk)
+
+        @pl.when(step >= 2)
+        def _():
+            for off_x in range(2):
+                some = far_ref.at[0, 0] if core_flip else kept_ref.at[0]
+                leaving(some, step, off_x).wait()
+
+        for off_x in range(2):
+            total = product[off_x]
+            if not core_flip:
+                fetched(step, off_x).wait()
+                total = total + got[step, off_x].astype(F32)
+            ready[slot, off_x] = total.astype(LOW)
+            first, second = spot(1 - step // parts, off_x)
+            if core_flip:
+                leaving(far_ref.at[first, second], step, off_x).start()
+            else:
+                for at, target in enumerate((kept_ref, sent_ref)):
+
+                    @pl.when(first == at)
+                    def _():
+                        leaving(target.at[second], step, off_x).start()
+
+        @pl.when(step == steps - 1)
+        def _():
+            for back in range(min(2, steps)):
+                for off_x in range(2):
+                    some = far_ref.at[0, 0] if core_flip else kept_ref.at[0]
+                    leaving(some, step - back, off_x).wait()
 
     def right_at(t, me):
-        first, second, part = spot(t)
-        off_y, _ = places(me[0], core_flip, first, second)
-        return 0, ((me[0] & 1) ^ off_y) * parts + part
-
-    def body(me_ref, turn_ref, right_ref, *refs):
-        step = pl.program_id(0)
-        first, second, _ = spot(step)
-        _, off_x = places(me_ref[0], core_flip, first, second)
-        lefts = refs[-1]
-        for off_z in range(depth):
-            row = pl.multiple_of(dp_of(me_ref[0], core_flip, off_x, off_z) * rows, rows)
-            lefts[off_z * rows : (off_z + 1) * rows, :] = turn_ref[pl.ds(row, rows), :]
-        product = mm(lefts[...], right_ref[...])
-        if core_flip:
-            refs[0][0, 0] = product.astype(LOW).reshape(depth, rows, chunk)
-            return
-        total = product.reshape(depth, rows, chunk) + refs[0][0, 0].astype(F32)
-        for at in range(2):
-
-            @pl.when(first == at)
-            def _():
-                refs[1 + at][0] = total.astype(LOW)
-
-    def both(t, me):
-        first, second, part = spot(t)
-        return first, second, 0, 0, part
-
-    def only(at):
-        def index(t, me):
-            first, second, part = spot(t)
-            idle_second, idle_part = (0, 0) if at == 0 else (1, parts - 1)
-            return (
-                jnp.where(first == at, second, idle_second),
-                0,
-                0,
-                jnp.where(first == at, part, idle_part),
-            )
-
-        return index
-
-    block5 = pl.BlockSpec((1, 1, depth, rows, chunk), both)
+        return 0, ((me[0] & 1) ^ (1 - t // parts)) * parts + t % parts
+
     ins = [whole(width, count), pl.BlockSpec((count, chunk), right_at)]
+    scratch = [
+        pltpu.VMEM((2 * quarter, count), LOW),
+        pltpu.VMEM((2, 2, depth, rows, chunk), LOW),
+        pltpu.SemaphoreType.DMA((2, 2)),
+    ]
     if core_flip:
-        outs = block5
+        outs = ANY
         shapes = jax.ShapeDtypeStruct((2, 2, depth, rows, span), LOW)
         extra = ()
     else:
-        ins = ins + [block5]
-        outs = [pl.BlockSpec((1, depth, rows, chunk), only(at)) for at in range(2)]
+        ins = ins + [ANY]
+        outs = [ANY, ANY]
         shapes = [jax.ShapeDtypeStruct((2, depth, rows, span), LOW)] * 2
         extra = (received,)
+        scratch += [
+            pltpu.VMEM((steps, 2, depth, rows, chunk), LOW),
+            pltpu.SemaphoreType.DMA((steps, 2)),
+        ]
     return call(
         body,
-        (4 * parts,),
+        (steps,),
         ins,
         outs,
         shapes,
-        [pltpu.VMEM((width // 4, count), LOW)],
+        scratch,
         2 * count * width * span,
         count * (width + span * 2) * 2 + width * span * 4,
         name,
@@ -572,35 +604,68 @@
     )
 
 
-def gather_pieces(piece, size, depth):
-    own = jnp.stack([piece] + [swap(piece, size, k << Z_SHIFT) for k in range(1, depth)])
-    first = swap(own, size, Y_BIT, X_BIT)
-    second = swap(own, size, X_BIT, Y_BIT)
-    both = swap(first, size, X_BIT, Y_BIT)
-    held = [own, second, first, both]
-    return held + [swap(value, size, CORE_BIT) for value in held]
-
-
-def gather_vectors(vector, size, depth, dp_rank):
-    dp_size = 4 * depth
-    held = jnp.stack([vector] + [swap(vector, size, k << Z_SHIFT) for k in range(1, depth)])
-    held = jnp.stack([held, swap(held, size, X_BIT)], axis=1)
-    held = jnp.stack([held, swap(held, size, CORE_BIT)], axis=2)
-    held = held.reshape(dp_size, -1)
-    spot = jnp.arange(dp_size)
-    pick = (spot[None, :] == (spot ^ dp_rank)[:, None]).astype(F32)
-    return jnp.matmul(pick, held, precision=lax.Precision.HIGHEST)
-
-
-def finish_scatter(kept, sent, size, depth):
-    received = swap(sent, size, Y_BIT, X_BIT)
-    total = (kept.astype(F32) + received.astype(F32)).astype(LOW)
-    received = swap(total[1], size, X_BIT, Y_BIT)
-    total = (total[0].astype(F32) + received.astype(F32)).astype(LOW)
-    result = total[0].astype(F32)
-    for k in range(1, depth):
-        result = result + swap(total[k], size, k << Z_SHIFT).astype(F32)
-    return result
+def after(value, *others):
+    return lax.optimization_barrier((value, *others))[0]
+
+
+def gather_depth(piece, size, depth):
+    return jnp.stack([piece] + [swap(piece, size, k << Z_SHIFT) for k in range(1, depth)])
+
+
+def along_first(value, size):
+    return swap(value, size, Y_BIT, X_BIT)
+
+
+def along_second(value, size):
+    return swap(value, size, X_BIT, Y_BIT)
+
+
+def along_core(value, size):
+    return swap(value, size, CORE_BIT)
+
+
+class Scatter:
+    def __init__(self, turned, right, size, depth, name):
+        self.size, self.depth, self.name = size, depth, name
+        self.turned, self.right = turned, right
+
+    def far(self, me):
+        self.me = me
+        self.sent = weight_grad_call(
+            me, self.turned, self.right, self.depth, 1, None, self.name + "_far"
+        )
+        self.received = swap(self.sent, self.size, CORE_BIT)
+        return self.sent
+
+    def near(self, *others):
+        right = after(self.right, *others)
+        self.kept, self.sent = weight_grad_call(
+            self.me, self.turned, right, self.depth, 0, self.received, self.name + "_near"
+        )
+        self.received = swap(self.sent, self.size, Y_BIT, X_BIT)
+        return self.kept
+
+    def second(self, *others):
+        kept = after(self.kept, *others)
+        total = (kept.astype(F32) + self.received.astype(F32)).astype(LOW)
+        self.kept = total[0]
+        self.received = swap(total[1], self.size, X_BIT, Y_BIT)
+        return self.kept
+
+    def third(self, *others):
+        kept = after(self.kept, *others)
+        total = (kept.astype(F32) + self.received.astype(F32)).astype(LOW)
+        self.kept = total[0]
+        self.received = [
+            swap(total[k], self.size, k << Z_SHIFT) for k in range(1, self.depth)
+        ]
+        return self.kept
+
+    def last(self, *others):
+        result = after(self.kept, *others).astype(F32)
+        for value in self.received:
+            result = result + value.astype(F32)
+        return result
 
 
 def sum_all(value, size, depth):
@@ -653,11 +718,24 @@
             fc1_bias,
         ]
     )
-    vector = jnp.pad(vector.astype(LOW).astype(F32), (0, -vector.shape[0] % 1024))
-    pieces_one = gather_pieces(piece_one, size, depth)
-    gathered = gather_vectors(vector.reshape(-1, TILE), size, depth, dp_rank)
-    pieces_two = gather_pieces(piece_two, size, depth)
-    pieces_three = gather_pieces(piece_three, size, depth)
+    vector = lax.optimization_barrier(vector).astype(LOW).astype(F32)
+
+    held_one = gather_depth(piece_one, size, depth)
+    gathered = lax.all_gather(vector, "dp", axis=0, tiled=False)
+    held_one, gathered = lax.optimization_barrier((held_one, gathered))
+    first_one = along_first(held_one, size)
+    second_one = along_second(held_one, size)
+    held_two = gather_depth(after(piece_two, held_one), size, depth)
+    first_one, second_one, held_two = lax.optimization_barrier((first_one, second_one, held_two))
+    both_one = along_second(first_one, size)
+    plane_one = [held_one, second_one, first_one]
+    pieces_one = [along_core(value, size) for value in plane_one]
+    both_one, *pieces_one = lax.optimization_barrier((both_one, *pieces_one))
+    pieces_one = plane_one + [both_one] + pieces_one + [along_core(both_one, size)]
+    *pieces_one, held_two = lax.optimization_barrier((*pieces_one, held_two))
+    first_two = along_first(held_two, size)
+    second_two = along_second(held_two, size)
+    held_three = gather_depth(after(piece_three, held_two), size, depth)
     table = gathered[:, : 8 * rows].reshape(dp_size, 8, rows).transpose(1, 0, 2).reshape(8, width)
     fc1_full = gathered[:, 8 * rows : 12 * rows].reshape(1, 4 * width)
     qkv_bias = jnp.stack(
@@ -671,34 +749,76 @@
     own_mask = lax.dynamic_slice_in_dim(key_mask, tensor_rank * own_images, own_images, 0)
     visible = jnp.concatenate(
         [jnp.ones((own_images, seq - key_mask.shape[1]), jnp.int32), own_mask], axis=1
-    )[:, None, :]
+    )
+    visible_rows = after(visible, held_one)[:, :, None]
+    visible = visible[:, None, :]
 
     normed_one, turned_one, qkv = qkv_call(me, rows_in, table, qkv_bias, pieces_one)
     mixed = attend_call(me, qkv, visible)
+    mixed, first_two, second_two, held_three = lax.optimization_barrier(
+        (mixed, first_two, second_two, held_three)
+    )
+    both_two = along_second(first_two, size)
+    plane_two = [held_two, second_two, first_two]
+    pieces_two = [along_core(value, size) for value in plane_two]
     middle, normed_two, turned_two = project_call(me, mixed, rows_in, table, pieces_one)
+    both_two, normed_two, *pieces_two = lax.optimization_barrier((both_two, normed_two, *pieces_two))
+    pieces_two = plane_two + [both_two] + pieces_two + [along_core(both_two, size)]
+    *pieces_two, held_three = lax.optimization_barrier((*pieces_two, held_three))
+    first_three = along_first(held_three, size)
+    second_three = along_second(held_three, size)
     hidden, slope = expand_call(me, normed_two, fc1_full, pieces_two)
-
-    def weight_grad(turned, right, name):
-        sent = weight_grad_call(me, turned, right, depth, 1, None, name + "_far")
-        received = swap(sent, size, CORE_BIT)
-        kept, sent = weight_grad_call(me, turned, right, depth, 0, received, name + "_near")
-        return finish_scatter(kept, sent, size, depth)
-
-    fc2_grad = weight_grad(out_turned, hidden, "fc2_grad")
+    hidden, first_three, second_three = lax.optimization_barrier(
+        (hidden, first_three, second_three)
+    )
+    both_three = along_second(first_three, size)
+    plane_three = [held_three, second_three, first_three]
+    pieces_three = [along_core(value, size) for value in plane_three]
+    fc2 = Scatter(out_turned, hidden, size, depth, "fc2_grad")
+    done = fc2.far(me)
+    done, both_three, *pieces_three = lax.optimization_barrier((done, both_three, *pieces_three))
+    pieces_three = plane_three + [both_three] + pieces_three + [along_core(both_three, size)]
     outputs, pre_low, fc1_sum = contract_call(
-        me, hidden, slope, out_low, middle, table, pieces_three
-    )
-    fc1_grad = weight_grad(turned_two, pre_low, "fc1_grad")
+        me, after(hidden, done), slope, out_low, middle, table, pieces_three
+    )
+    done = fc2.near(pre_low)
+    fc1 = Scatter(turned_two, after(pre_low, done), size, depth, "fc1_grad")
+    done = fc1.far(me)
     middle_grad, vec_two, middle_low, turned_mid = norm_back_call(
-        me, pre_low, 0, 5, middle, grad_in, table, pieces_two, True, "norm_two_back"
-    )
-    proj_grad = weight_grad(turned_mid, mixed, "proj_grad")
-    mixed_grad = mixed_back_call(me, middle_low, pieces_one)
-    qkv_low, qkv_sum = attend_back_call(me, qkv, mixed_grad, visible)
-    qkv_grad = weight_grad(turned_one, qkv_low, "qkv_grad")
+        me, after(pre_low, done), 0, 5, middle, grad_in, table, pieces_two, True, "norm_two_back"
+    )
+    done = fc2.second(middle_low)
+    done = fc1.near(done)
+    done = fc2.third(done)
+    mixed_grad = mixed_back_call(me, after(middle_low, done), pieces_one)
+    proj = Scatter(turned_mid, after(mixed, mixed_grad), size, depth, "proj_grad")
+    done = proj.far(me)
+    qkv_low, qkv_sum = attend_back_call(me, qkv, after(mixed_grad, done), visible_rows)
+    done = proj.near(qkv_low)
+    done = fc1.second(done)
+    qkv_out = Scatter(turned_one, after(qkv_low, done), size, depth, "qkv_grad")
+    done = qkv_out.far(me)
+    done = fc1.third(proj.second(done))
+    fc2_grad = fc2.last(done)
+    done = qkv_out.near(fc2_grad)
     input_grad, vec_one = norm_back_call(
-        me, qkv_low, 0, 0, rows_in, middle_grad, table, pieces_one, False, "norm_one_back"
-    )
+        me,
+        after(qkv_low, done),
+        0,
+        0,
+        rows_in,
+        middle_grad,
+        table,
+        pieces_one,
+        False,
+        "norm_one_back",
+    )
+    proj.third(input_grad)
+    qkv_out.second(input_grad)
+    qkv_out.third()
+    fc1_grad = fc1.last()
+    proj_grad = proj.last()
+    qkv_grad = qkv_out.last()
 
     qkv_sum = jnp.sum(qkv_sum, axis=(0, 2)).reshape(2, 3, half)
     sums = jnp.concatenate(

time: 527 us -> 434 us (0.82)
  Pallas kernels: 214 us -> 139 us
  waiting for transfers between devices: 184 us -> 118 us
  local copies, waits for them, and re-layouts: 21.1 us -> 56.8 us
  blocking collectives: 0 us -> 28.3 us
  starting transfers between devices: 81.8 us -> 68.4 us
    ppermute x65 -> x60, waiting for transfers between devices: 184 us -> 118 us  [swap(): lax.ppermute(value, AXES, [(i, i ^ (other if i & CORE_BIT else bits)) for...]
    unnamed x58 -> x182, local copies, waits for them, and re-layouts: 5.14 us -> 43.8 us
    pallas_call x8, Pallas kernels: 73.2 us -> 37.9 us  [weight_grad_call(): call(body, (steps,), ins, outs, shapes, scratch, 2 * count * width * span...]
    all_gather x0 -> x1, blocking collectives: none -> 28.3 us  [shards(): gathered = lax.all_gather(vector, 'dp', axis=0, tiled=False)]
    ppermute x65 -> x60, starting transfers between devices: 81.8 us -> 68.4 us  [swap(): lax.ppermute(value, AXES, [(i, i ^ (other if i & CORE_BIT else bits)) for...]
    pallas_call x2, Pallas kernels: 33.6 us -> 24.1 us  [norm_back_call(): call(body, (4,), [pl.BlockSpec((count, chunk), lambda t, me: (0, t)), who...]
    pallas_call x1, Pallas kernels: 18.3 us -> 10.9 us  [attend_call(): call(body, (images, 2), [pl.BlockSpec((seq, 3 * half), lambda i, y, me: (...]
    pallas_call x1, Pallas kernels: 27.6 us -> 20.2 us  [attend_back_call(): call(body, (images, 2), [pl.BlockSpec((seq, 3 * half), lambda i, y, me: (...]
  transfers between devices with their start and end apart: 65 -> 60, of which waited for: 25 -> 21; matrix products, arithmetic and copies ran while one was open for 7% -> 6% of each run, Pallas kernels for 25% -> 26%
where the time goes in v2:
time: 434 us; the launch traced here: 431 us
  Pallas kernels  139 us (32%)
  waiting for transfers between devices  118 us (27%)
  starting transfers between devices  68.4 us (16%)
  local copies, waits for them, and re-layouts  56.8 us (13%)
  blocking collectives  28.3 us (7%)
  other arithmetic  18.5 us (4%)
    ppermute x60, waiting for transfers between devices, swap(): lax.ppermute(value, AXES, [(i, i ^ (other if i & CORE_BIT else bits)) for...  118 us
    ppermute x60, starting transfers between devices, swap(): lax.ppermute(value, AXES, [(i, i ^ (other if i & CORE_BIT else bits)) for...  68.4 us
    unnamed x182, local copies, waits for them, and re-layouts  43.8 us
    pallas_call x8, Pallas kernels, weight_grad_call(): call(body, (steps,), ins, outs, shapes, scratch, 2 * count * width * span...  37.9 us
    all_gather x1, blocking collectives, shards(): gathered = lax.all_gather(vector, 'dp', axis=0, tiled=False)  28.3 us
    pallas_call x2, Pallas kernels, norm_back_call(): call(body, (4,), [pl.BlockSpec((count, chunk), lambda t, me: (0, t)), who...  24.1 us
    pallas_call x1, Pallas kernels, attend_back_call(): call(body, (images, 2), [pl.BlockSpec((seq, 3 * half), lambda i, y, me: (...  20.2 us
    pallas_call x1, Pallas kernels, contract_call(): call(body, (8,), [part, part, whole(count, width), whole(count, width), w...  17.4 us
  transfers between devices with their start and end apart: 60, of which 21 were waited for; matrix products, arithmetic and copies ran while one was open for 6% of the time, Pallas kernels for 26%

profile of v2, /device:TPU:0, one launch (start us, length us, event | category | flops | bytes accessed | tf_op | source)
XLA Modules:
  0.0 430.6 jit_solution(6089096160687769718)
XLA Ops:
  2.7 3.1 collective-permute-start
  5.8 2.6 collective-permute-start.1
  10.0 28.3 %all-gather.1 = f32[16,1,768]{2,1,0:T(1,128)S(1)} all-gather(f32[1,1,768]{2,1,0:T(1,128)S(1)} %reshape.136), channel_id=2, replica_groups=mesh['dp'=16,'tensor'=2] {'dp'}, dimensions={0}, use_global_device_ids=true | all-gather | bytes 52224 | tf_op jit(solution)/shard_map/all_gather | solution.py:724
  41.7 3.7 collective-permute-start.5
  47.8 8.6 %collective-permute-done.5 = bf16[64,2048]{1,0:T(8,128)(2,1)S(1)} collective-permute-done((bf16[64,2048]{1,0:T(8,128)(2,1)S(1)}, bf16[64,2048]{1,0:T(8,128)(2,1)S(1)}, u32[]{:S(2)}, u32[]{:S(2)}) %collective-permute-start.5) | collective-permute-done | bytes 262176 | tf_op jit(solution)/shard_map/ppermute | solution.py:602
  56.5 10.3 %collective-permute-done.6 = bf16[64,2048]{1,0:T(8,128)(2,1)S(1)} collective-permute-done((bf16[64,2048]{1,0:T(8,128)(2,1)S(1)}, bf16[64,2048]{1,0:T(8,128)(2,1)S(1)}, u32[]{:S(2)}, u32[]{:S(2)}) %collective-permute-start.6) | collective-permute-done | bytes 262176 | tf_op jit(solution)/shard_map/ppermute | solution.py:602
  71.5 11.4 %collective-permute-done.8.refs_3_ = bf16[4,64,2048]{2,1,0:T(8,128)(2,1)} collective-permute-done((bf16[4,64,2048]{2,1,0:T(8,128)(2,1)S(1)}, bf16[4,64,2048]{2,1,0:T(8,128)(2,1)}, u32[]{:S(2)}, u32[]{:S(2)}) %collective-permute-start.8) | collective-permute-done | bytes 1048608 | tf_op jit(solution)/shard_map/ppermute | solution.py:602
  89.5 4.8 %collective-permute-start.15 = (bf16[64,2048]{1,0:T(8,128)(2,1)S(1)}, bf16[64,2048]{1,0:T(8,128)(2,1)S(1)}, u32[]{:S(2)}, u32[]{:S(2)}) collective-permute-start(bf16[64,2048]{1,0:T(8,128)(2,1)S(1)} %convert_bitcast_fusion), channel_id=1, source_target_pairs={{0,8},{1,9},{2,10},{3,11},{4,12},{5,13},{6,14},{7,15},{8,0},{9,1},... | collective-permute-start | bytes 786440 | tf_op jit(solution)/shard_map/ppermute | solution.py:602
  102.2 9.1 %qkv.1 = (bf16[640,1024]{1,0:T(8,128)(2,1)}, bf16[1024,640]{1,0:T(8,128)(2,1)S(1)}, bf16[640,3072]{1,0:T(8,128)(2,1)S(1)}) custom-call(s32[1]{0:T(128)} %bitcast.me_ref, f32[640,1024]{1,0:T(8,128)S(1)} %bitcast.121, f32[8,1024]{1,0:T(8,128)S(1)} %reshape.124.table_ref, f32[1,3072]{1,0:T(1,128)S(1)} %reshape.125.bias_ref, ...), custom_call_target="tpu_custom_call" | custom-call | flops 4026531840 | bytes 16777216 | tf_op jit(solution)/shard_map/qkv/pallas_call | solution.py:121
  111.3 10.9 %attend.1.mixed_ref.right_ref = bf16[640,1024]{1,0:T(8,128)(2,1)S(1)} custom-call(s32[1]{0:T(128)} %bitcast.me_ref, bf16[640,3072]{1,0:T(8,128)(2,1)S(1)} %get-tuple-element.123.qkv_ref, s32[2,1,320]{2,1,0:T(1,128)S(1)} %broadcast_in_dim.10.seen_ref), custom_call_target="tpu_custom_call" | custom-call | flops 3355443200 | bytes 5898240 | tf_op jit(solution)/shard_map/attend/pallas_call | solution.py:169
  125.7 4.0 project.1
  131.9 6.7 %collective-permute-done.18.refs_3_ = bf16[4,64,2048]{2,1,0:T(8,128)(2,1)S(1)} collective-permute-done((bf16[4,64,2048]{2,1,0:T(8,128)(2,1)}, bf16[4,64,2048]{2,1,0:T(8,128)(2,1)S(1)}, u32[]{:S(2)}, u32[]{:S(2)}) %collective-permute-start.18) | collective-permute-done | bytes 1048608 | tf_op jit(solution)/shard_map/ppermute | solution.py:602
  157.4 12.6 %expand.1 = (bf16[640,4096]{1,0:T(8,128)(2,1)S(1)}, bf16[640,4096]{1,0:T(8,128)(2,1)S(1)}) custom-call(s32[1]{0:T(128)} %bitcast.me_ref, bf16[640,1024]{1,0:T(8,128)(2,1)S(1)} %copy-done.61, f32[1,4096]{1,0:T(1,128)S(1)} %bitcast.126, bf16[4,64,2048]{2,1,0:T(8,128)(2,1)S(1)} %copy-done.55, bf16[4,64,2048]{2,1,0:T(8,128)(2,1)} %collective-permute-done.14.refs_1_, ...), custom_call_target="tpu_custom_call" | custom-call | flops 5368709120 | bytes 18874368 | tf_op jit(solution)/shard_map/expand/pallas_call | solution.py:249
  170.1 2.3 copy-done.79
  172.4 6.0 %fc2_grad_far.1 = bf16[2,2,4,64,2048]{4,3,2,1,0:T(8,128)(2,1)} custom-call(s32[1]{0:T(128)} %bitcast.me_ref, bf16[1024,640]{1,0:T(8,128)(2,1)S(1)} %copy-done.10, bf16[640,4096]{1,0:T(8,128)(2,1)S(1)} %get-tuple-element.158.right_ref.hid_ref), custom_call_target="tpu_custom_call" | custom-call | flops 2684354560 | bytes 14942208 | tf_op jit(solution)/shard_map/fc2_grad_far/pallas_call | solution.py:587
  179.9 7.5 %collective-permute-done.26.refs_4_ = bf16[4,64,2048]{2,1,0:T(8,128)(2,1)S(1)} collective-permute-done((bf16[4,64,2048]{2,1,0:T(8,128)(2,1)}, bf16[4,64,2048]{2,1,0:T(8,128)(2,1)S(1)}, u32[]{:S(2)}, u32[]{:S(2)}) %collective-permute-start.26) | collective-permute-done | bytes 1048608 | tf_op jit(solution)/shard_map/ppermute | solution.py:602
  187.3 6.7 %collective-permute-done.25.refs_3_ = bf16[4,64,2048]{2,1,0:T(8,128)(2,1)S(1)} collective-permute-done((bf16[4,64,2048]{2,1,0:T(8,128)(2,1)}, bf16[4,64,2048]{2,1,0:T(8,128)(2,1)S(1)}, u32[]{:S(2)}, u32[]{:S(2)}) %collective-permute-start.25) | collective-permute-done | bytes 1048608 | tf_op jit(solution)/shard_map/ppermute | solution.py:602
  194.0 2.7 collective-permute-done.29.refs_7_
  196.6 17.4 %contract.1 = (f32[640,1024]{1,0:T(8,128)}, bf16[640,4096]{1,0:T(8,128)(2,1)S(1)}, f32[1,4096]{1,0:T(1,128)S(1)}) custom-call(s32[1]{0:T(128)} %bitcast.me_ref, bf16[640,4096]{1,0:T(8,128)(2,1)S(1)} %get-tuple-element.158.right_ref.hid_ref, bf16[640,4096]{1,0:T(8,128)(2,1)} %copy-done.79, bf16[640,1024]{1,0:T(8,128)(2,1)S(1)} %copy-done.35, ...), custom_call_target="tpu_custom_call" | custom-call | flops 10737418240 | bytes 24117248 | tf_op jit(solution)/shard_map/contract/pallas_call | solution.py:290
  214.1 6.1 %fc2_grad_near.1 = (bf16[2,4,64,2048]{3,2,1,0:T(8,128)(2,1)S(1)}, bf16[2,4,64,2048]{3,2,1,0:T(8,128)(2,1)}) custom-call(s32[1]{0:T(128)} %bitcast.me_ref, bf16[1024,640]{1,0:T(8,128)(2,1)S(1)} %copy-done.10, bf16[640,4096]{1,0:T(8,128)(2,1)S(1)} %get-tuple-element.158.right_ref.hid_ref, bf16[2,2,4,64,2048]{4,3,2,1,0:T(8,128)(2,1)S(1)} %collective-permute-done.30.refs_0_), custom_call_target="tpu_custom_call" | custom-call | flops 2684354560 | bytes 14942208 | tf_op jit(solution)/shard_map/fc2_grad_near/pallas_call | solution.py:587
  220.3 5.3 %fc1_grad_far.1 = bf16[2,2,4,64,2048]{4,3,2,1,0:T(8,128)(2,1)S(1)} custom-call(s32[1]{0:T(128)} %bitcast.me_ref, bf16[1024,640]{1,0:T(8,128)(2,1)S(1)} %copy-done.41, bf16[640,4096]{1,0:T(8,128)(2,1)S(1)} %get-tuple-element.165.right_ref.low_ref), custom_call_target="tpu_custom_call" | custom-call | flops 2684354560 | bytes 14942208 | tf_op jit(solution)/shard_map/fc1_grad_far/pallas_call | solution.py:587
  229.3 12.8 %norm_two_back.1 = (f32[640,1024]{1,0:T(8,128)S(1)}, f32[8,1024]{1,0:T(8,128)S(1)}, bf16[640,1024]{1,0:T(8,128)(2,1)S(1)}, bf16[1024,640]{1,0:T(8,128)(2,1)S(1)}) custom-call(s32[1]{0:T(128)} %bitcast.me_ref, bf16[640,4096]{1,0:T(8,128)(2,1)} %copy-done.4, f32[640,1024]{1,0:T(8,128)S(1)} %copy-done.59, f32[640,1024]{1,0:T(8,128)S(1)} %bitcast.125, ...), custom_call_target="tpu_custom_call" | custom-call | flops 5368709120 | bytes 24117248 | tf_op jit(solution)/shard_map/norm_two_back/pallas_call | solution.py:374
  242.2 11.2 %collective-permute-done.31 = bf16[2,4,64,2048]{3,2,1,0:T(8,128)(2,1)} collective-permute-done((bf16[2,4,64,2048]{3,2,1,0:T(8,128)(2,1)}, bf16[2,4,64,2048]{3,2,1,0:T(8,128)(2,1)}, u32[]{:S(2)}, u32[]{:S(2)}) %collective-permute-start.31) | collective-permute-done | bytes 2097184 | tf_op jit(solution)/shard_map/ppermute | solution.py:602
  253.4 2.5 add_convert_fusion.1
  256.5 6.1 %fc1_grad_near.1 = (bf16[2,4,64,2048]{3,2,1,0:T(8,128)(2,1)S(1)}, bf16[2,4,64,2048]{3,2,1,0:T(8,128)(2,1)}) custom-call(s32[1]{0:T(128)} %bitcast.me_ref, bf16[1024,640]{1,0:T(8,128)(2,1)S(1)} %copy-done.41, bf16[640,4096]{1,0:T(8,128)(2,1)S(1)} %copy-done.5, bf16[2,2,4,64,2048]{4,3,2,1,0:T(8,128)(2,1)S(1)} %collective-permute-done.32.refs_0_), custom_call_target="tpu_custom_call" | custom-call | flops 2684354560 | bytes 14942208 | tf_op jit(solution)/shard_map/fc1_grad_near/pallas_call | solution.py:587
  263.3 13.0 %collective-permute-done.33 = bf16[4,64,2048]{2,1,0:T(8,128)(2,1)S(1)} collective-permute-done((bf16[4,64,2048]{2,1,0:T(8,128)(2,1)S(1)}, bf16[4,64,2048]{2,1,0:T(8,128)(2,1)S(1)}, u32[]{:S(2)}, u32[]{:S(2)}) %collective-permute-start.33) | collective-permute-done | bytes 1048608 | tf_op jit(solution)/shard_map/ppermute | solution.py:602
  277.8 2.4 mixed_back.1.grad_ref
  280.2 2.3 proj_grad_far.1
  285.8 2.1 copy-done.78
  287.9 20.2 %attend_back.1 = (bf16[640,3072]{1,0:T(8,128)(2,1)S(1)}, f32[2,2,1,1536]{3,2,1,0:T(1,128)S(1)}) custom-call(s32[1]{0:T(128)} %bitcast.me_ref, bf16[640,3072]{1,0:T(8,128)(2,1)S(1)} %copy-done.78, bf16[640,1024]{1,0:T(8,128)(2,1)S(1)} %copy-done.53, s32[2,320,1]{2,1,0:T(8,128)S(1)} %copy-done.56), custom_call_target="tpu_custom_call" | custom-call | flops 8388608000 | bytes 9830400 | tf_op jit(solution)/shard_map/attend_back/pallas_call | solution.py:461
  308.1 3.2 proj_grad_near.1
  311.4 2.5 add_convert_fusion
  315.2 4.2 qkv_grad_far.1
  323.8 11.4 %collective-permute-done.36 = bf16[2,4,64,512]{3,2,1,0:T(8,128)(2,1)S(1)} collective-permute-done((bf16[2,4,64,512]{3,2,1,0:T(8,128)(2,1)S(1)}, bf16[2,4,64,512]{3,2,1,0:T(8,128)(2,1)S(1)}, u32[]{:S(2)}, u32[]{:S(2)}) %collective-permute-start.36) | collective-permute-done | bytes 524320 | tf_op jit(solution)/shard_map/ppermute | solution.py:602
  335.1 2.4 collective-permute-start.40
  341.1 2.6 collective-permute-done.40
  344.6 4.8 %qkv_grad_near.1 = (bf16[2,4,64,1536]{3,2,1,0:T(8,128)(2,1)S(1)}, bf16[2,4,64,1536]{3,2,1,0:T(8,128)(2,1)}) custom-call(s32[1]{0:T(128)} %bitcast.me_ref, bf16[1024,640]{1,0:T(8,128)(2,1)S(1)} %copy-done.39, bf16[640,3072]{1,0:T(8,128)(2,1)S(1)} %get-tuple-element.186.right_ref.low_ref, bf16[2,2,4,64,1536]{4,3,2,1,0:T(8,128)(2,1)S(1)} %collective-permute-done.41.refs_0_), custom_call_target="tpu_custom_call" | custom-call | flops 2013265920 | bytes 11534336 | tf_op jit(solution)/shard_map/qkv_grad_near/pallas_call | solution.py:587
  350.5 2.2 collective-permute-start.48
  354.5 4.8 %collective-permute-start.57 = (bf16[64,2048]{1,0:T(8,128)(2,1)}, bf16[64,2048]{1,0:T(8,128)(2,1)}, u32[]{:S(2)}, u32[]{:S(2)}) collective-permute-start(bf16[64,2048]{1,0:T(8,128)(2,1)} %get-tuple-element.234), channel_id=1, source_target_pairs={{0,8},{1,9},{2,10},{3,11},{4,12},{5,13},{6,14},{7,15},{8,0},{9,1},... | collective-permute-start | bytes 786440 | tf_op jit(solution)/shard_map/ppermute | solution.py:602
  361.6 2.1 copy-done.3
  370.9 11.3 %norm_one_back.1 = (f32[640,1024]{1,0:T(8,128)}, f32[8,1024]{1,0:T(8,128)S(1)}) custom-call(s32[1]{0:T(128)} %bitcast.me_ref, bf16[640,3072]{1,0:T(8,128)(2,1)S(1)} %copy-done.3, f32[640,1024]{1,0:T(8,128)S(1)} %bitcast.123, f32[640,1024]{1,0:T(8,128)S(1)} %copy-done.43, f32[8,1024]{1,0:T(8,128)S(1)} %reshape.124.table_ref, ...), custom_call_target="tpu_custom_call" | custom-call | flops 4026531840 | bytes 20709376 | tf_op jit(solution)/shard_map/norm_one_back/pallas_call | solution.py:374
  382.4 2.2 convert_add_fusion
  396.1 2.1 collective-permute-start.46
  398.2 1.9 add_convert_fusion.2
  407.7 6.1 %collective-permute-done.49 = bf16[4,64,1536]{2,1,0:T(8,128)(2,1)S(1)} collective-permute-done((bf16[4,64,1536]{2,1,0:T(8,128)(2,1)S(1)}, bf16[4,64,1536]{2,1,0:T(8,128)(2,1)S(1)}, u32[]{:S(2)}, u32[]{:S(2)}) %collective-permute-start.49) | collective-permute-done | bytes 786464 | tf_op jit(solution)/shard_map/ppermute | solution.py:602
  414.1 2.9 collective-permute-start.51
  419.0 4.0 collective-permute-done.50
  423.1 6.1 %collective-permute-done.51 = bf16[64,1536]{1,0:T(8,128)(2,1)S(1)} collective-permute-done((bf16[64,1536]{1,0:T(8,128)(2,1)S(1)}, bf16[64,1536]{1,0:T(8,128)(2,1)S(1)}, u32[]{:S(2)}, u32[]{:S(2)}) %collective-permute-start.51) | collective-permute-done | bytes 196640 | tf_op jit(solution)/shard_map/ppermute | solution.py:602
  (336 shorter events, 109.4 us)
Async XLA Ops:
  2.7 35.6 %collective-permute-start = (bf16[64,2048]{1,0:T(8,128)(2,1)S(1)}, bf16[64,2048]{1,0:T(8,128)(2,1)S(1)}, u32[]{:S(2)}, u32[]{:S(2)}) collective-permute-start(bf16[64,2048]{1,0:T(8,128)(2,1)S(1)} %pad_maximum_fusion.3), channel_id=1, source_target_pairs={{0,8},{1,9},{2,10},{3,11},{4,12},{5,13},{6,14},{7,15},{8,0},{9,1},... | collective-permute-start | bytes 786440 | tf_op jit(solution)/shard_map/ppermute | solution.py:602
  5.8 32.5 %collective-permute-start.1 = (bf16[64,2048]{1,0:T(8,128)(2,1)S(1)}, bf16[64,2048]{1,0:T(8,128)(2,1)S(1)}, u32[]{:S(2)}, u32[]{:S(2)}) collective-permute-start(bf16[64,2048]{1,0:T(8,128)(2,1)S(1)} %pad_maximum_fusion.3), channel_id=1, source_target_pairs={{0,16},{1,17},{2,18},{3,19},{4,20},{5,21},{6,22},{7,23},{8,24},{9,... | collective-permute-start | bytes 786440 | tf_op jit(solution)/shard_map/ppermute | solution.py:602
  8.4 29.9 %collective-permute-start.2 = (bf16[64,2048]{1,0:T(8,128)(2,1)S(1)}, bf16[64,2048]{1,0:T(8,128)(2,1)S(1)}, u32[]{:S(2)}, u32[]{:S(2)}) collective-permute-start(bf16[64,2048]{1,0:T(8,128)(2,1)S(1)} %pad_maximum_fusion.3), channel_id=1, source_target_pairs={{0,24},{1,25},{2,26},{3,27},{4,28},{5,29},{6,30},{7,31},{8,16},{9,... | collective-permute-start | bytes 786440 | tf_op jit(solution)/shard_map/ppermute | solution.py:602
  38.5 29.4 %collective-permute-start.3 = (bf16[4,64,2048]{2,1,0:T(8,128)(2,1)S(1)}, bf16[4,64,2048]{2,1,0:T(8,128)(2,1)S(1)}, u32[]{:S(2)}, u32[]{:S(2)}) collective-permute-start(bf16[4,64,2048]{2,1,0:T(8,128)(2,1)S(1)} %pad_maximum_fusion.refs_0_), channel_id=1, source_target_pairs={{0,1},{1,0},{2,6},{3,7},{4,5},{5,4},{6,2},{7,3},{8,9},{9,8},{10,14... | collective-permute-start | bytes 3145736 | tf_op jit(solution)/shard_map/ppermute | solution.py:602
  40.1 27.8 %collective-permute-start.4 = (bf16[4,64,2048]{2,1,0:T(8,128)(2,1)S(1)}, bf16[4,64,2048]{2,1,0:T(8,128)(2,1)S(1)}, u32[]{:S(2)}, u32[]{:S(2)}) collective-permute-start(bf16[4,64,2048]{2,1,0:T(8,128)(2,1)S(1)} %pad_maximum_fusion.refs_0_), channel_id=1, source_target_pairs={{0,4},{1,5},{2,3},{3,2},{4,0},{5,1},{6,7},{7,6},{8,12},{9,13},{10,... | collective-permute-start | bytes 3145736 | tf_op jit(solution)/shard_map/ppermute | solution.py:602
  41.7 14.8 %collective-permute-start.5 = (bf16[64,2048]{1,0:T(8,128)(2,1)S(1)}, bf16[64,2048]{1,0:T(8,128)(2,1)S(1)}, u32[]{:S(2)}, u32[]{:S(2)}) collective-permute-start(bf16[64,2048]{1,0:T(8,128)(2,1)S(1)} %convert_element_type.145), channel_id=1, source_target_pairs={{0,8},{1,9},{2,10},{3,11},{4,12},{5,13},{6,14},{7,15},{8,0},{9,1},... | collective-permute-start | bytes 786440 | tf_op jit(solution)/shard_map/ppermute | solution.py:602
  45.4 21.3 %collective-permute-start.6 = (bf16[64,2048]{1,0:T(8,128)(2,1)S(1)}, bf16[64,2048]{1,0:T(8,128)(2,1)S(1)}, u32[]{:S(2)}, u32[]{:S(2)}) collective-permute-start(bf16[64,2048]{1,0:T(8,128)(2,1)S(1)} %convert_element_type.145), channel_id=1, source_target_pairs={{0,16},{1,17},{2,18},{3,19},{4,20},{5,21},{6,22},{7,23},{8,24},{9,... | collective-permute-start | bytes 786440 | tf_op jit(solution)/shard_map/ppermute | solution.py:602
  46.9 19.9 %collective-permute-start.7 = (bf16[64,2048]{1,0:T(8,128)(2,1)S(1)}, bf16[64,2048]{1,0:T(8,128)(2,1)S(1)}, u32[]{:S(2)}, u32[]{:S(2)}) collective-permute-start(bf16[64,2048]{1,0:T(8,128)(2,1)S(1)} %convert_element_type.145), channel_id=1, source_target_pairs={{0,24},{1,25},{2,26},{3,27},{4,28},{5,29},{6,30},{7,31},{8,16},{9,... | collective-permute-start | bytes 786440 | tf_op jit(solution)/shard_map/ppermute | solution.py:602
  56.5 12.2 %collective-permute-start.9 = (bf16[4,64,2048]{2,1,0:T(8,128)(2,1)S(1)}, bf16[4,64,2048]{2,1,0:T(8,128)(2,1)S(1)}, u32[]{:S(2)}, u32[]{:S(2)}) collective-permute-start(bf16[4,64,2048]{2,1,0:T(8,128)(2,1)S(1)} %pad_maximum_fusion.refs_0_), channel_id=1, source_target_pairs={{0,2},{1,3},{2,0},{3,1},{4,6},{5,7},{6,4},{7,5},{8,10},{9,11},{10,... | collective-permute-start | bytes 3145736 | tf_op jit(solution)/shard_map/ppermute | solution.py:602
  67.9 15.0 %collective-permute-start.8 = (bf16[4,64,2048]{2,1,0:T(8,128)(2,1)S(1)}, bf16[4,64,2048]{2,1,0:T(8,128)(2,1)}, u32[]{:S(2)}, u32[]{:S(2)}) collective-permute-start(bf16[4,64,2048]{2,1,0:T(8,128)(2,1)S(1)} %collective-permute-done.3.refs_2_), channel_id=1, source_target_pairs={{0,4},{1,5},{2,3},{3,2},{4,0},{5,1},{6,7},{7,6},{8,12},{9,13},{10,... | collective-permute-start | bytes 3145736 | tf_op jit(solution)/shard_map/ppermute | solution.py:602
  68.4 14.5 %collective-permute-start.10 = (bf16[4,64,2048]{2,1,0:T(8,128)(2,1)S(1)}, bf16[4,64,2048]{2,1,0:T(8,128)(2,1)S(1)}, u32[]{:S(2)}, u32[]{:S(2)}) collective-permute-start(bf16[4,64,2048]{2,1,0:T(8,128)(2,1)S(1)} %collective-permute-done.4.refs_1_), channel_id=1, source_target_pairs={{0,2},{1,3},{2,0},{3,1},{4,6},{5,7},{6,4},{7,5},{8,10},{9,11},{10,... | collective-permute-start | bytes 3145736 | tf_op jit(solution)/shard_map/ppermute | solution.py:602
  87.0 36.5 %collective-permute-start.13 = (bf16[4,64,2048]{2,1,0:T(8,128)(2,1)}, bf16[4,64,2048]{2,1,0:T(8,128)(2,1)}, u32[]{:S(2)}, u32[]{:S(2)}) collective-permute-start(bf16[4,64,2048]{2,1,0:T(8,128)(2,1)} %pad_maximum_fusion.1.refs_0_), channel_id=1, source_target_pairs={{0,1},{1,0},{2,6},{3,7},{4,5},{5,4},{6,2},{7,3},{8,9},{9,8},{10,14... | collective-permute-start | bytes 3145736 | tf_op jit(solution)/shard_map/ppermute | solution.py:602
  87.5 36.0 %collective-permute-start.14 = (bf16[4,64,2048]{2,1,0:T(8,128)(2,1)}, bf16[4,64,2048]{2,1,0:T(8,128)(2,1)}, u32[]{:S(2)}, u32[]{:S(2)}) collective-permute-start(bf16[4,64,2048]{2,1,0:T(8,128)(2,1)} %pad_maximum_fusion.1.refs_0_), channel_id=1, source_target_pairs={{0,4},{1,5},{2,3},{3,2},{4,0},{5,1},{6,7},{7,6},{8,12},{9,13},{10,... | collective-permute-start | bytes 3145736 | tf_op jit(solution)/shard_map/ppermute | solution.py:602
  89.5 32.7 %collective-permute-start.15 = (bf16[64,2048]{1,0:T(8,128)(2,1)S(1)}, bf16[64,2048]{1,0:T(8,128)(2,1)S(1)}, u32[]{:S(2)}, u32[]{:S(2)}) collective-permute-start(bf16[64,2048]{1,0:T(8,128)(2,1)S(1)} %convert_bitcast_fusion), channel_id=1, source_target_pairs={{0,8},{1,9},{2,10},{3,11},{4,12},{5,13},{6,14},{7,15},{8,0},{9,1},... | collective-permute-start | bytes 786440 | tf_op jit(solution)/shard_map/ppermute | solution.py:602
  94.3 28.1 %collective-permute-start.16 = (bf16[64,2048]{1,0:T(8,128)(2,1)S(1)}, bf16[64,2048]{1,0:T(8,128)(2,1)S(1)}, u32[]{:S(2)}, u32[]{:S(2)}) collective-permute-start(bf16[64,2048]{1,0:T(8,128)(2,1)S(1)} %convert_bitcast_fusion), channel_id=1, source_target_pairs={{0,16},{1,17},{2,18},{3,19},{4,20},{5,21},{6,22},{7,23},{8,24},{9,... | collective-permute-start | bytes 786440 | tf_op jit(solution)/shard_map/ppermute | solution.py:602
  95.3 27.1 %collective-permute-start.17 = (bf16[64,2048]{1,0:T(8,128)(2,1)S(1)}, bf16[64,2048]{1,0:T(8,128)(2,1)S(1)}, u32[]{:S(2)}, u32[]{:S(2)}) collective-permute-start(bf16[64,2048]{1,0:T(8,128)(2,1)S(1)} %convert_bitcast_fusion), channel_id=1, source_target_pairs={{0,24},{1,25},{2,26},{3,27},{4,28},{5,29},{6,30},{7,31},{8,16},{9,... | collective-permute-start | bytes 786440 | tf_op jit(solution)/shard_map/ppermute | solution.py:602
  123.5 15.1 %collective-permute-start.18 = (bf16[4,64,2048]{2,1,0:T(8,128)(2,1)}, bf16[4,64,2048]{2,1,0:T(8,128)(2,1)S(1)}, u32[]{:S(2)}, u32[]{:S(2)}) collective-permute-start(bf16[4,64,2048]{2,1,0:T(8,128)(2,1)} %collective-permute-done.13.refs_2_), channel_id=1, source_target_pairs={{0,4},{1,5},{2,3},{3,2},{4,0},{5,1},{6,7},{7,6},{8,12},{9,13},{10,... | collective-permute-start | bytes 3145736 | tf_op jit(solution)/shard_map/ppermute | solution.py:602
  125.2 13.4 %collective-permute-start.20 = (bf16[4,64,2048]{2,1,0:T(8,128)(2,1)}, bf16[4,64,2048]{2,1,0:T(8,128)(2,1)S(1)}, u32[]{:S(2)}, u32[]{:S(2)}) collective-permute-start(bf16[4,64,2048]{2,1,0:T(8,128)(2,1)} %collective-permute-done.14.refs_1_), channel_id=1, source_target_pairs={{0,2},{1,3},{2,0},{3,1},{4,6},{5,7},{6,4},{7,5},{8,10},{9,11},{10,... | collective-permute-start | bytes 3145736 | tf_op jit(solution)/shard_map/ppermute | solution.py:602
  125.3 14.3 %collective-permute-start.21 = (bf16[4,64,2048]{2,1,0:T(8,128)(2,1)}, bf16[4,64,2048]{2,1,0:T(8,128)(2,1)S(1)}, u32[]{:S(2)}, u32[]{:S(2)}) collective-permute-start(bf16[4,64,2048]{2,1,0:T(8,128)(2,1)} %collective-permute-done.13.refs_2_), channel_id=1, source_target_pairs={{0,2},{1,3},{2,0},{3,1},{4,6},{5,7},{6,4},{7,5},{8,10},{9,11},{10,... | collective-permute-start | bytes 3145736 | tf_op jit(solution)/shard_map/ppermute | solution.py:602
  144.2 28.2 %collective-permute-start.23 = (bf16[4,64,2048]{2,1,0:T(8,128)(2,1)}, bf16[4,64,2048]{2,1,0:T(8,128)(2,1)}, u32[]{:S(2)}, u32[]{:S(2)}) collective-permute-start(bf16[4,64,2048]{2,1,0:T(8,128)(2,1)} %pad_maximum_fusion.2.refs_0_), channel_id=1, source_target_pairs={{0,1},{1,0},{2,6},{3,7},{4,5},{5,4},{6,2},{7,3},{8,9},{9,8},{10,14... | collective-permute-start | bytes 3145736 | tf_op jit(solution)/shard_map/ppermute | solution.py:602
  145.7 26.7 %collective-permute-start.24 = (bf16[4,64,2048]{2,1,0:T(8,128)(2,1)}, bf16[4,64,2048]{2,1,0:T(8,128)(2,1)}, u32[]{:S(2)}, u32[]{:S(2)}) collective-permute-start(bf16[4,64,2048]{2,1,0:T(8,128)(2,1)} %pad_maximum_fusion.2.refs_0_), channel_id=1, source_target_pairs={{0,4},{1,5},{2,3},{3,2},{4,0},{5,1},{6,7},{7,6},{8,12},{9,13},{10,... | collective-permute-start | bytes 3145736 | tf_op jit(solution)/shard_map/ppermute | solution.py:602
  178.4 35.7 %collective-permute-start.30 = (bf16[2,2,4,64,2048]{4,3,2,1,0:T(8,128)(2,1)}, bf16[2,2,4,64,2048]{4,3,2,1,0:T(8,128)(2,1)S(1)}, u32[]{:S(2)}, u32[]{:S(2)}) collective-permute-start(bf16[2,2,4,64,2048]{4,3,2,1,0:T(8,128)(2,1)} %fc2_grad_far.1), channel_id=1, source_target_pairs={{0,2},{1,3},{2,0},{3,1},{4,6},{5,7},{6,4},{7,5},{8,10},{9,11},{10,... | collective-permute-start | bytes 12582920 | tf_op jit(solution)/shard_map/ppermute | solution.py:602
  178.5 8.9 %collective-permute-start.26 = (bf16[4,64,2048]{2,1,0:T(8,128)(2,1)}, bf16[4,64,2048]{2,1,0:T(8,128)(2,1)S(1)}, u32[]{:S(2)}, u32[]{:S(2)}) collective-permute-start(bf16[4,64,2048]{2,1,0:T(8,128)(2,1)} %pad_maximum_fusion.2.refs_0_), channel_id=1, source_target_pairs={{0,2},{1,3},{2,0},{3,1},{4,6},{5,7},{6,4},{7,5},{8,10},{9,11},{10,... | collective-permute-start | bytes 3145736 | tf_op jit(solution)/shard_map/ppermute | solution.py:602
  178.9 15.0 %collective-permute-start.25 = (bf16[4,64,2048]{2,1,0:T(8,128)(2,1)}, bf16[4,64,2048]{2,1,0:T(8,128)(2,1)S(1)}, u32[]{:S(2)}, u32[]{:S(2)}) collective-permute-start(bf16[4,64,2048]{2,1,0:T(8,128)(2,1)} %collective-permute-done.23.refs_2_), channel_id=1, source_target_pairs={{0,4},{1,5},{2,3},{3,2},{4,0},{5,1},{6,7},{7,6},{8,12},{9,13},{10,... | collective-permute-start | bytes 3145736 | tf_op jit(solution)/shard_map/ppermute | solution.py:602
  179.3 14.6 %collective-permute-start.27 = (bf16[4,64,2048]{2,1,0:T(8,128)(2,1)}, bf16[4,64,2048]{2,1,0:T(8,128)(2,1)S(1)}, u32[]{:S(2)}, u32[]{:S(2)}) collective-permute-start(bf16[4,64,2048]{2,1,0:T(8,128)(2,1)} %collective-permute-done.24.refs_1_), channel_id=1, source_target_pairs={{0,2},{1,3},{2,0},{3,1},{4,6},{5,7},{6,4},{7,5},{8,10},{9,11},{10,... | collective-permute-start | bytes 3145736 | tf_op jit(solution)/shard_map/ppermute | solution.py:602
  179.6 14.4 %collective-permute-start.28 = (bf16[4,64,2048]{2,1,0:T(8,128)(2,1)}, bf16[4,64,2048]{2,1,0:T(8,128)(2,1)S(1)}, u32[]{:S(2)}, u32[]{:S(2)}) collective-permute-start(bf16[4,64,2048]{2,1,0:T(8,128)(2,1)} %collective-permute-done.23.refs_2_), channel_id=1, source_target_pairs={{0,2},{1,3},{2,0},{3,1},{4,6},{5,7},{6,4},{7,5},{8,10},{9,11},{10,... | collective-permute-start | bytes 3145736 | tf_op jit(solution)/shard_map/ppermute | solution.py:602
  225.6 30.9 %collective-permute-start.32 = (bf16[2,2,4,64,2048]{4,3,2,1,0:T(8,128)(2,1)S(1)}, bf16[2,2,4,64,2048]{4,3,2,1,0:T(8,128)(2,1)S(1)}, u32[]{:S(2)}, u32[]{:S(2)}) collective-permute-start(bf16[2,2,4,64,2048]{4,3,2,1,0:T(8,128)(2,1)S(1)} %fc1_grad_far.1), channel_id=1, source_target_pairs={{0,2},{1,3},{2,0},{3,1},{4,6},{5,7},{6,4},{7,5},{8,10},{9,11},{10,... | collective-permute-start | bytes 12582920 | tf_op jit(solution)/shard_map/ppermute | solution.py:602
  227.0 26.4 %collective-permute-start.31 = (bf16[2,4,64,2048]{3,2,1,0:T(8,128)(2,1)}, bf16[2,4,64,2048]{3,2,1,0:T(8,128)(2,1)}, u32[]{:S(2)}, u32[]{:S(2)}) collective-permute-start(bf16[2,4,64,2048]{3,2,1,0:T(8,128)(2,1)} %get-tuple-element.164), channel_id=1, source_target_pairs={{0,1},{1,0},{2,6},{3,7},{4,5},{5,4},{6,2},{7,3},{8,9},{9,8},{10,14... | collective-permute-start | bytes 6291464 | tf_op jit(solution)/shard_map/ppermute | solution.py:602
  256.1 20.3 %collective-permute-start.33 = (bf16[4,64,2048]{2,1,0:T(8,128)(2,1)S(1)}, bf16[4,64,2048]{2,1,0:T(8,128)(2,1)S(1)}, u32[]{:S(2)}, u32[]{:S(2)}) collective-permute-start(bf16[4,64,2048]{2,1,0:T(8,128)(2,1)S(1)} %get-tuple-element.231), channel_id=1, source_target_pairs={{0,4},{1,5},{2,3},{3,2},{4,0},{5,1},{6,7},{7,6},{8,12},{9,13},{10,... | collective-permute-start | bytes 3145736 | tf_op jit(solution)/shard_map/ppermute | solution.py:602
  262.7 48.5 %collective-permute-start.35 = (bf16[2,4,64,2048]{3,2,1,0:T(8,128)(2,1)}, bf16[2,4,64,2048]{3,2,1,0:T(8,128)(2,1)}, u32[]{:S(2)}, u32[]{:S(2)}) collective-permute-start(bf16[2,4,64,2048]{3,2,1,0:T(8,128)(2,1)} %get-tuple-element.178), channel_id=1, source_target_pairs={{0,1},{1,0},{2,6},{3,7},{4,5},{5,4},{6,2},{7,3},{8,9},{9,8},{10,14... | collective-permute-start | bytes 6291464 | tf_op jit(solution)/shard_map/ppermute | solution.py:602
  282.5 25.6 %collective-permute-start.34 = (bf16[2,2,4,64,512]{4,3,2,1,0:T(8,128)(2,1)}, bf16[2,2,4,64,512]{4,3,2,1,0:T(8,128)(2,1)}, u32[]{:S(2)}, u32[]{:S(2)}) collective-permute-start(bf16[2,2,4,64,512]{4,3,2,1,0:T(8,128)(2,1)} %proj_grad_far.1), channel_id=1, source_target_pairs={{0,2},{1,3},{2,0},{3,1},{4,6},{5,7},{6,4},{7,5},{8,10},{9,11},{10,... | collective-permute-start | bytes 3145736 | tf_op jit(solution)/shard_map/ppermute | solution.py:602
  319.4 25.2 %collective-permute-start.41 = (bf16[2,2,4,64,1536]{4,3,2,1,0:T(8,128)(2,1)S(1)}, bf16[2,2,4,64,1536]{4,3,2,1,0:T(8,128)(2,1)S(1)}, u32[]{:S(2)}, u32[]{:S(2)}) collective-permute-start(bf16[2,2,4,64,1536]{4,3,2,1,0:T(8,128)(2,1)S(1)} %qkv_grad_far.1), channel_id=1, source_target_pairs={{0,2},{1,3},{2,0},{3,1},{4,6},{5,7},{6,4},{7,5},{8,10},{9,11},{10,... | collective-permute-start | bytes 9437192 | tf_op jit(solution)/shard_map/ppermute | solution.py:602
  319.9 19.8 %collective-permute-start.37 = (bf16[4,64,2048]{2,1,0:T(8,128)(2,1)S(1)}, bf16[4,64,2048]{2,1,0:T(8,128)(2,1)S(1)}, u32[]{:S(2)}, u32[]{:S(2)}) collective-permute-start(bf16[4,64,2048]{2,1,0:T(8,128)(2,1)S(1)} %get-tuple-element.228), channel_id=1, source_target_pairs={{0,4},{1,5},{2,3},{3,2},{4,0},{5,1},{6,7},{7,6},{8,12},{9,13},{10,... | collective-permute-start | bytes 3145736 | tf_op jit(solution)/shard_map/ppermute | solution.py:602
  320.3 14.8 %collective-permute-start.36 = (bf16[2,4,64,512]{3,2,1,0:T(8,128)(2,1)S(1)}, bf16[2,4,64,512]{3,2,1,0:T(8,128)(2,1)S(1)}, u32[]{:S(2)}, u32[]{:S(2)}) collective-permute-start(bf16[2,4,64,512]{3,2,1,0:T(8,128)(2,1)S(1)} %get-tuple-element.181), channel_id=1, source_target_pairs={{0,1},{1,0},{2,6},{3,7},{4,5},{5,4},{6,2},{7,3},{8,9},{9,8},{10,14... | collective-permute-start | bytes 1572872 | tf_op jit(solution)/shard_map/ppermute | solution.py:602
  320.8 20.2 %collective-permute-start.38 = (bf16[64,2048]{1,0:T(8,128)(2,1)S(1)}, bf16[64,2048]{1,0:T(8,128)(2,1)S(1)}, u32[]{:S(2)}, u32[]{:S(2)}) collective-permute-start(bf16[64,2048]{1,0:T(8,128)(2,1)S(1)} %copy-done.84), channel_id=1, source_target_pairs={{0,8},{1,9},{2,10},{3,11},{4,12},{5,13},{6,14},{7,15},{8,0},{9,1},... | collective-permute-start | bytes 786440 | tf_op jit(solution)/shard_map/ppermute | solution.py:602
  321.9 19.2 %collective-permute-start.39 = (bf16[64,2048]{1,0:T(8,128)(2,1)S(1)}, bf16[64,2048]{1,0:T(8,128)(2,1)S(1)}, u32[]{:S(2)}, u32[]{:S(2)}) collective-permute-start(bf16[64,2048]{1,0:T(8,128)(2,1)S(1)} %copy-done.83), channel_id=1, source_target_pairs={{0,16},{1,17},{2,18},{3,19},{4,20},{5,21},{6,22},{7,23},{8,24},{9,... | collective-permute-start | bytes 786440 | tf_op jit(solution)/shard_map/ppermute | solution.py:602
  350.5 45.6 %collective-permute-start.48 = (bf16[2,4,64,1536]{3,2,1,0:T(8,128)(2,1)}, bf16[2,4,64,1536]{3,2,1,0:T(8,128)(2,1)}, u32[]{:S(2)}, u32[]{:S(2)}) collective-permute-start(bf16[2,4,64,1536]{3,2,1,0:T(8,128)(2,1)} %get-tuple-element.194), channel_id=1, source_target_pairs={{0,1},{1,0},{2,6},{3,7},{4,5},{5,4},{6,2},{7,3},{8,9},{9,8},{10,14... | collective-permute-start | bytes 4718600 | tf_op jit(solution)/shard_map/ppermute | solution.py:602
  354.0 32.3 %collective-permute-start.53 = (bf16[4,64,512]{2,1,0:T(8,128)(2,1)}, bf16[4,64,512]{2,1,0:T(8,128)(2,1)}, u32[]{:S(2)}, u32[]{:S(2)}) collective-permute-start(bf16[4,64,512]{2,1,0:T(8,128)(2,1)} %get-tuple-element.246), channel_id=1, source_target_pairs={{0,4},{1,5},{2,3},{3,2},{4,0},{5,1},{6,7},{7,6},{8,12},{9,13},{10,... | collective-permute-start | bytes 786440 | tf_op jit(solution)/shard_map/ppermute | solution.py:602
  354.5 27.8 %collective-permute-start.57 = (bf16[64,2048]{1,0:T(8,128)(2,1)}, bf16[64,2048]{1,0:T(8,128)(2,1)}, u32[]{:S(2)}, u32[]{:S(2)}) collective-permute-start(bf16[64,2048]{1,0:T(8,128)(2,1)} %get-tuple-element.234), channel_id=1, source_target_pairs={{0,8},{1,9},{2,10},{3,11},{4,12},{5,13},{6,14},{7,15},{8,0},{9,1},... | collective-permute-start | bytes 786440 | tf_op jit(solution)/shard_map/ppermute | solution.py:602
  359.2 23.1 %collective-permute-start.58 = (bf16[64,2048]{1,0:T(8,128)(2,1)}, bf16[64,2048]{1,0:T(8,128)(2,1)}, u32[]{:S(2)}, u32[]{:S(2)}) collective-permute-start(bf16[64,2048]{1,0:T(8,128)(2,1)} %get-tuple-element.236), channel_id=1, source_target_pairs={{0,16},{1,17},{2,18},{3,19},{4,20},{5,21},{6,22},{7,23},{8,24},{9,... | collective-permute-start | bytes 786440 | tf_op jit(solution)/shard_map/ppermute | solution.py:602
  360.1 22.2 %collective-permute-start.59 = (bf16[64,2048]{1,0:T(8,128)(2,1)}, bf16[64,2048]{1,0:T(8,128)(2,1)}, u32[]{:S(2)}, u32[]{:S(2)}) collective-permute-start(bf16[64,2048]{1,0:T(8,128)(2,1)} %get-tuple-element.235), channel_id=1, source_target_pairs={{0,24},{1,25},{2,26},{3,27},{4,28},{5,29},{6,30},{7,31},{8,16},{9,... | collective-permute-start | bytes 786440 | tf_op jit(solution)/shard_map/ppermute | solution.py:602
  390.7 9.5 %collective-permute-start.54 = (bf16[64,512]{1,0:T(8,128)(2,1)S(1)}, bf16[64,512]{1,0:T(8,128)(2,1)S(1)}, u32[]{:S(2)}, u32[]{:S(2)}) collective-permute-start(bf16[64,512]{1,0:T(8,128)(2,1)S(1)} %get-tuple-element.254), channel_id=1, source_target_pairs={{0,8},{1,9},{2,10},{3,11},{4,12},{5,13},{6,14},{7,15},{8,0},{9,1},... | collective-permute-start | bytes 196616 | tf_op jit(solution)/shard_map/ppermute | solution.py:602
  392.4 9.4 %collective-permute-start.55 = (bf16[64,512]{1,0:T(8,128)(2,1)S(1)}, bf16[64,512]{1,0:T(8,128)(2,1)S(1)}, u32[]{:S(2)}, u32[]{:S(2)}) collective-permute-start(bf16[64,512]{1,0:T(8,128)(2,1)S(1)} %get-tuple-element.253), channel_id=1, source_target_pairs={{0,16},{1,17},{2,18},{3,19},{4,20},{5,21},{6,22},{7,23},{8,24},{9,... | collective-permute-start | bytes 196616 | tf_op jit(solution)/shard_map/ppermute | solution.py:602
  393.7 9.3 %collective-permute-start.56 = (bf16[64,512]{1,0:T(8,128)(2,1)S(1)}, bf16[64,512]{1,0:T(8,128)(2,1)S(1)}, u32[]{:S(2)}, u32[]{:S(2)}) collective-permute-start(bf16[64,512]{1,0:T(8,128)(2,1)S(1)} %get-tuple-element.252), channel_id=1, source_target_pairs={{0,24},{1,25},{2,26},{3,27},{4,28},{5,29},{6,30},{7,31},{8,16},{9,... | collective-permute-start | bytes 196616 | tf_op jit(solution)/shard_map/ppermute | solution.py:602
  401.8 12.0 %collective-permute-start.49 = (bf16[4,64,1536]{2,1,0:T(8,128)(2,1)S(1)}, bf16[4,64,1536]{2,1,0:T(8,128)(2,1)S(1)}, u32[]{:S(2)}, u32[]{:S(2)}) collective-permute-start(bf16[4,64,1536]{2,1,0:T(8,128)(2,1)S(1)} %get-tuple-element.233), channel_id=1, source_target_pairs={{0,4},{1,5},{2,3},{3,2},{4,0},{5,1},{6,7},{7,6},{8,12},{9,13},{10,... | collective-permute-start | bytes 2359304 | tf_op jit(solution)/shard_map/ppermute | solution.py:602
  414.0 9.0 %collective-permute-start.50 = (bf16[64,1536]{1,0:T(8,128)(2,1)S(1)}, bf16[64,1536]{1,0:T(8,128)(2,1)S(1)}, u32[]{:S(2)}, u32[]{:S(2)}) collective-permute-start(bf16[64,1536]{1,0:T(8,128)(2,1)S(1)} %get-tuple-element.245), channel_id=1, source_target_pairs={{0,8},{1,9},{2,10},{3,11},{4,12},{5,13},{6,14},{7,15},{8,0},{9,1},... | collective-permute-start | bytes 589832 | tf_op jit(solution)/shard_map/ppermute | solution.py:602
  414.1 15.0 %collective-permute-start.51 = (bf16[64,1536]{1,0:T(8,128)(2,1)S(1)}, bf16[64,1536]{1,0:T(8,128)(2,1)S(1)}, u32[]{:S(2)}, u32[]{:S(2)}) collective-permute-start(bf16[64,1536]{1,0:T(8,128)(2,1)S(1)} %get-tuple-element.244), channel_id=1, source_target_pairs={{0,16},{1,17},{2,18},{3,19},{4,20},{5,21},{6,22},{7,23},{8,24},{9,... | collective-permute-start | bytes 589832 | tf_op jit(solution)/shard_map/ppermute | solution.py:602
  417.0 12.1 %collective-permute-start.52 = (bf16[64,1536]{1,0:T(8,128)(2,1)S(1)}, bf16[64,1536]{1,0:T(8,128)(2,1)S(1)}, u32[]{:S(2)}, u32[]{:S(2)}) collective-permute-start(bf16[64,1536]{1,0:T(8,128)(2,1)S(1)} %get-tuple-element.243), channel_id=1, source_target_pairs={{0,24},{1,25},{2,26},{3,27},{4,28},{5,29},{6,30},{7,31},{8,16},{9,... | collective-permute-start | bytes 589832 | tf_op jit(solution)/shard_map/ppermute | solution.py:602
  (98 other events, 1076.7 us)
